TPU v7x, 256 devices: a whole 4x4x8 slice. The times are simulated.
256 devices in a mesh: tm: 32 (over x_lo, z, core), space: 8 (over x_hi, y).
Axes of the slice: x: 4 (x_hi: 2, x_lo: 2; x = x_hi * 2 + x_lo), y: 4, z: 8, core: 2. Of those that a mesh axis runs over, the one named last changes fastest.
Arguments:
- start_disp: float32 [32, 3, 4, 256, 256], P('tm', None, None, 'space'), may hold values from -0.2 to 0.2
- start_vel: float32 [32, 3, 4, 256, 256], P('tm', None, None, 'space'), may hold values from -0.2 to 0.2
- start_visc: float32 [32, 3, 4, 256, 256], P('tm', None, None, 'space'), may hold values from -0.2 to 0.2
- init_state: float32 [3, 3, 4, 256, 256], P(None, None, None, 'space'), may hold values from -0.2 to 0.2
- inv_mass: float32 [4, 256, 256], P(None, 'space'), may hold values from 0.35 to 1
- damping_rate: float32 [4, 256, 256], P(None, 'space'), may hold values from 0.002 to 0.2
- visc_rate: float32 [4, 256, 256], P(None, 'space'), may hold values from 0.02 to 2
- fiber_stiff: float32 [4, 256, 256], P(None, 'space'), may hold values from 0.05 to 0.25
- fiber_family: int32 [64, 8], P('space'), may hold values from 0 to 3
- pressure: float32 [32, 4], P('tm'), may hold values from 0.2 to 1
Outputs:
- new_disp: float32 [32, 3, 4, 256, 256], P('tm', None, None, 'space')
- new_vel: float32 [32, 3, 4, 256, 256], P('tm', None, None, 'space')
- new_visc: float32 [32, 3, 4, 256, 256], P('tm', None, None, 'space')
All inputs are finite; a program needn't handle non-finite values.
Results may differ from a plain program's by a relative error of at most 0.000029.
Values sent between devices are 32-bit elements; how exact they have to be, the bound alone decides.
A program may use at most 128 MiB of HBM per device.

v0:
```python
import math

import jax
import jax.numpy as jnp
from jax import lax
from jax.sharding import Mesh
from jax.sharding import PartitionSpec as P

STEPS = 4
BLK_AX = 4
BLK_CIR = 32
TM = ("tm_0", "tm_1", "tm_2")


COEF_AXIAL = 0.22
COEF_CIRC = 0.22
COEF_RADIAL = 0.12
VISC_SHARE = 0.6
TIME_STEP = 1.0
FIBER_ANGLES = (0.5, -0.5, 0.9, -0.9)


def with_halo(cells, sides, width):
    for axis, dim in sides:
        count = lax.axis_size(axis)
        ends = count - 1
        head = lax.slice_in_dim(cells, 0, width, axis=dim)
        tail = lax.slice_in_dim(cells, cells.shape[dim] - width, cells.shape[dim], axis=dim)
        cells = jnp.concatenate(
            [
                lax.ppermute(tail, axis, [(i, (i + 1) % count) for i in range(ends)]),
                cells,
                lax.ppermute(head, axis, [((i + 1) % count, i) for i in range(ends)]),
            ],
            axis=dim,
        )
    return cells


def from_behind(value, axis, steps):
    count = lax.axis_size(axis)
    leading, last = (max(0, -steps), min(count, count - steps))
    return lax.ppermute(value, axis, [(source, source + steps) for source in range(leading, last)])


def filled_with(shard, identity):
    return jax.tree.map(
        lambda part, zero: jnp.zeros_like(part) + jnp.asarray(zero, part.dtype), shard, identity
    )


def entering(shard, axes, combine, identity):
    before = start = filled_with(shard, identity)
    running = shard
    for axis in reversed(axes):
        size, position = (lax.axis_size(axis), lax.axis_index(axis))
        pieces = jax.tree.map(lambda part: lax.all_gather(part, axis), running)
        inside, running = (start, start)
        for k in range(size):
            passed = k < position
            running = combine(running, jax.tree.map(lambda part: part[k], pieces))
            inside = jax.tree.map(lambda new, old: jnp.where(passed, new, old), running, inside)
        before = combine(inside, before)
    return before


def directions(fiber_family, block_rows, block_cols):
    count_a, count_c = fiber_family.shape
    spread = jnp.broadcast_to(
        fiber_family[:, None, :, None], (count_a, block_rows, count_c, block_cols)
    )
    spread = spread.reshape(count_a * block_rows, count_c * block_cols)
    cosine = jnp.zeros(spread.shape, jnp.float32)
    sine_part = jnp.zeros(spread.shape, jnp.float32)
    for family, radians in enumerate(FIBER_ANGLES):
        chosen = jnp.where(spread == family, 1.0, 0.0).astype(jnp.float32)
        cosine = cosine + chosen * math.cos(radians)
        sine_part = sine_part + chosen * math.sin(radians)
    return (cosine, sine_part)


def materials(fiber_stiff, fiber_family):
    cosine, sine_part = directions(fiber_family, BLK_AX, BLK_CIR)
    return jnp.stack(
        [
            fiber_stiff,
            jnp.broadcast_to(cosine, fiber_stiff.shape),
            jnp.broadcast_to(sine_part, fiber_stiff.shape),
        ]
    )


def stencil(u_pad, mat_pad):
    center = u_pad[:, :, 1:-1]
    axial = u_pad[:, :, 2:] + u_pad[:, :, :-2] - 2.0 * center
    circle = jnp.roll(center, 1, 3) + jnp.roll(center, -1, 3) - 2.0 * center
    radial_pad = jnp.pad(center, ((0, 0), (1, 1), (0, 0), (0, 0)))
    radial = radial_pad[:, 2:] + radial_pad[:, :-2] - 2.0 * center
    elastic = COEF_AXIAL * axial + COEF_CIRC * circle + COEF_RADIAL * radial
    grad_axial = u_pad[:, :, 1:] - u_pad[:, :, :-1]
    lower = u_pad[:, :, :-1]
    grad_circ = jnp.roll(lower, -1, 3) - lower
    stiffness = mat_pad[0, :, :-1]
    cosine = mat_pad[1, :, :-1]
    sine_part = mat_pad[2, :, :-1]
    strain = (
        cosine * cosine * grad_axial[1]
        + sine_part * sine_part * grad_circ[2]
        + cosine * sine_part * (grad_axial[2] + grad_circ[1])
    )
    weight = jnp.exp(strain * strain)
    sigma = stiffness * weight * strain
    axial_one = sigma * cosine * cosine
    mixed = sigma * cosine * sine_part
    circ_two = sigma * sine_part * sine_part
    own_mixed = mixed[:, 1:]
    own_circ = circ_two[:, 1:]
    force_one = axial_one[:, 1:] - axial_one[:, :-1] + (own_mixed - jnp.roll(own_mixed, 1, 2))
    force_two = mixed[:, 1:] - mixed[:, :-1] + (own_circ - jnp.roll(own_circ, 1, 2))
    fiber = jnp.stack([jnp.zeros_like(force_one), force_one, force_two])
    return (elastic + fiber, elastic, weight[:, 1:])


def fine_step(state, u_pad, mat_pad, inv_mass, damping_rate, decay_factor, pressure_now):
    displace, velocity, viscous = state
    force_total, elastic, weight = stencil(u_pad, mat_pad)
    inner_wall = jnp.zeros((3, displace.shape[1], 1, 1), jnp.float32).at[0, 0].set(1.0)
    load_total = force_total + viscous + pressure_now * inner_wall
    acceleration = inv_mass * load_total - damping_rate * velocity
    next_vel = velocity + TIME_STEP * acceleration
    next_disp = displace + TIME_STEP * next_vel
    next_visc = decay_factor * viscous + (1.0 - decay_factor) * VISC_SHARE * elastic
    return ((next_disp, next_vel, next_visc), weight)


def coarse_matrix(inv_mass, damping_rate, fiber_stiff, weight):
    half_step = 0.5 * STEPS * TIME_STEP
    stiffness = inv_mass * (
        2.0 * (COEF_AXIAL + COEF_CIRC + COEF_RADIAL) + 2.0 * fiber_stiff * weight
    )
    damping_part = half_step * damping_rate
    square_part = half_step * half_step * stiffness
    determinant = 1.0 + damping_part + square_part
    return jnp.stack(
        [
            (1.0 + damping_part - square_part) / determinant,
            2.0 * half_step / determinant,
            -2.0 * half_step * stiffness / determinant,
            (1.0 - damping_part - square_part) / determinant,
        ]
    )


def relax(
    start, mat_pad, inv_mass, damping_rate, decay_factor, fiber_stiff, pressure_row, pad_field
):
    state = start
    first_weight = None
    for section in range(STEPS):
        u_pad = pad_field(state[0])
        state, weight = fine_step(
            state, u_pad, mat_pad, inv_mass, damping_rate, decay_factor, pressure_row[section]
        )
        if section == 0:
            first_weight = weight
    return (state, coarse_matrix(inv_mass, damping_rate, fiber_stiff, first_weight))


def apply_map(gmat, pair):
    return jnp.stack([gmat[0] * pair[0] + gmat[1] * pair[1], gmat[2] * pair[0] + gmat[3] * pair[1]])


def compose(latter, earlier):
    return jnp.stack(
        [
            latter[0] * earlier[0] + latter[1] * earlier[2],
            latter[0] * earlier[1] + latter[1] * earlier[3],
            latter[2] * earlier[0] + latter[3] * earlier[2],
            latter[2] * earlier[1] + latter[3] * earlier[3],
        ]
    )


def combine(earlier, latter):
    return (compose(latter[0], earlier[0]), apply_map(latter[0], earlier[1]) + latter[1])


def face_pad(field):
    return with_halo(field, (("space", 2),), 1)


def shards(
    start_disp,
    start_vel,
    start_visc,
    init_state,
    inv_mass,
    damping_rate,
    visc_rate,
    fiber_stiff,
    fiber_family,
    pressure,
):
    own_mat = materials(fiber_stiff, fiber_family)
    before = from_behind(own_mat[:, :, -1:], "space", 1)
    mat_pad = jnp.concatenate([before, own_mat, jnp.zeros_like(before)], 2)
    decay_factor = jnp.exp(-TIME_STEP * visc_rate)
    starts = jnp.stack([start_disp[0], start_vel[0], start_visc[0]])
    state, gmat = relax(
        (starts[0], starts[1], starts[2]),
        mat_pad,
        inv_mass,
        damping_rate,
        decay_factor,
        fiber_stiff,
        pressure[0],
        face_pad,
    )
    ends = jnp.stack([state[0], state[1], state[2]])
    arrived = from_behind(ends, TM, 1)
    first_slab = lax.axis_index(TM) == 0
    prior = jnp.where(first_slab, init_state, arrived)
    resid = prior[:2] - starts[:2]
    image = apply_map(gmat, resid)
    ones_field = jnp.ones_like(gmat[0])
    zero_field = jnp.zeros_like(gmat[0])
    identity = (jnp.stack([ones_field, zero_field, zero_field, ones_field]), jnp.zeros_like(image))
    prefix = entering((gmat, image), TM, combine, identity)
    error = prefix[1]
    new_disp = prior[0] + error[0]
    new_vel = prior[1] + error[1]
    return (new_disp[None], new_vel[None], prior[2][None])


def solution(mesh):
    finer = Mesh(
        mesh.devices.reshape(2, 8, 2, mesh.shape["space"]), ("tm_0", "tm_1", "tm_2", "space")
    )
    placed = (
        P(TM, None, None, "space", None),
        P(TM, None, None, "space", None),
        P(TM, None, None, "space", None),
        P(None, None, None, "space", None),
        P(None, "space", None),
        P(None, "space", None),
        P(None, "space", None),
        P(None, "space", None),
        P("space", None),
        P(TM, None),
    )
    return jax.shard_map(
        shards,
        mesh=finer,
        in_specs=placed,
        out_specs=(
            P(TM, None, None, "space", None),
            P(TM, None, None, "space", None),
            P(TM, None, None, "space", None),
        ),
        check_vma=False,
    )
```

profile of v0, /device:TPU:7, one launch (start us, length us, event | category | flops | bytes accessed | tf_op | source)
XLA Modules:
  0.0 316.1 jit_solution(6757942562632409852)
XLA Ops:
  8.2 3.2 %collective-permute-start.1 = (f32[3,4,1,256]{3,2,1,0:T(1,128)S(1)}, f32[3,4,1,256]{3,2,1,0:T(1,128)S(1)}, u32[]{:S(2)}, u32[]{:S(2)}) collective-permute-start(f32[3,4,1,256]{3,2,1,0:T(1,128)S(1)} %get-tuple-element.230), channel_id=1, source_target_pairs={{0,1},{1,2},{2,3},{3,4},{4,5},{5,6},{6,7},{8,9},{9,10},{10,11},{11... | collective-permute-start | bytes 36872 | tf_op jit(solution)/shard_map/ppermute | solution.py:31
  11.4 5.7 %collective-permute-start = (f32[3,4,1,256]{3,2,1,0:T(1,128)S(1)}, f32[3,4,1,256]{3,2,1,0:T(1,128)S(1)}, u32[]{:S(2)}, u32[]{:S(2)}) collective-permute-start(f32[3,4,1,256]{3,2,1,0:T(1,128)S(1)} %get-tuple-element.229), channel_id=1, source_target_pairs={{1,0},{2,1},{3,2},{4,3},{5,4},{6,5},{7,6},{9,8},{10,9},{11,10},{12... | collective-permute-start | bytes 36872 | tf_op jit(solution)/shard_map/ppermute | solution.py:33
  19.1 2.1 collective-permute-start.2
  22.1 2.5 broadcast_multiply_fusion
  24.8 2.4 collective-permute-done.2
  29.6 1.9 collective-permute-start.4
  31.6 7.0 %collective-permute-start.3 = (f32[3,4,1,256]{3,2,1,0:T(1,128)S(1)}, f32[3,4,1,256]{3,2,1,0:T(1,128)S(1)}, u32[]{:S(2)}, u32[]{:S(2)}) collective-permute-start(f32[3,4,1,256]{3,2,1,0:T(1,128)S(1)} %get-tuple-element.223), channel_id=1, source_target_pairs={{1,0},{2,1},{3,2},{4,3},{5,4},{6,5},{7,6},{9,8},{10,9},{11,10},{12... | collective-permute-start | bytes 36872 | tf_op jit(solution)/shard_map/ppermute | solution.py:33
  40.9 1.9 collective-permute-start.6
  42.9 7.2 %collective-permute-start.5 = (f32[3,4,1,256]{3,2,1,0:T(1,128)S(1)}, f32[3,4,1,256]{3,2,1,0:T(1,128)S(1)}, u32[]{:S(2)}, u32[]{:S(2)}) collective-permute-start(f32[3,4,1,256]{3,2,1,0:T(1,128)S(1)} %get-tuple-element.217), channel_id=1, source_target_pairs={{1,0},{2,1},{3,2},{4,3},{5,4},{6,5},{7,6},{9,8},{10,9},{11,10},{12... | collective-permute-start | bytes 36872 | tf_op jit(solution)/shard_map/ppermute | solution.py:33
  52.5 1.9 collective-permute-start.8
  54.6 7.2 %collective-permute-start.7 = (f32[3,4,1,256]{3,2,1,0:T(1,128)S(1)}, f32[3,4,1,256]{3,2,1,0:T(1,128)S(1)}, u32[]{:S(2)}, u32[]{:S(2)}) collective-permute-start(f32[3,4,1,256]{3,2,1,0:T(1,128)S(1)} %get-tuple-element.211), channel_id=1, source_target_pairs={{1,0},{2,1},{3,2},{4,3},{5,4},{6,5},{7,6},{9,8},{10,9},{11,10},{12... | collective-permute-start | bytes 36872 | tf_op jit(solution)/shard_map/ppermute | solution.py:33
  64.1 9.2 %collective-permute-start.9 = (f32[3,3,4,32,256]{4,3,2,1,0:T(8,128)S(1)}, f32[3,3,4,32,256]{4,3,2,1,0:T(8,128)}, u32[]{:S(2)}, u32[]{:S(2)}) collective-permute-start(f32[3,3,4,32,256]{4,3,2,1,0:T(8,128)S(1)} %pad_maximum_fusion), channel_id=1, source_target_pairs={{0,8},{8,16},{16,24},{24,32},{32,40},{40,48},{48,56},{56,64},{64,7... | collective-permute-start | bytes 3538952 | tf_op jit(solution)/shard_map/ppermute | solution.py:43
  74.5 12.0 %collective-permute-done.9 = f32[3,3,4,32,256]{4,3,2,1,0:T(8,128)} collective-permute-done((f32[3,3,4,32,256]{4,3,2,1,0:T(8,128)S(1)}, f32[3,3,4,32,256]{4,3,2,1,0:T(8,128)}, u32[]{:S(2)}, u32[]{:S(2)}) %collective-permute-start.9) | collective-permute-done | bytes 1179680 | tf_op jit(solution)/shard_map/ppermute | solution.py:43
  95.4 15.2 %all-gather.21.cloned.1.call-done = f32[4,3,4,32,256]{4,3,2,1,0:T(8,128)} async-done(((f32[2,3,4,32,256]{4,3,2,1,0:T(8,128)}), f32[4,3,4,32,256]{4,3,2,1,0:T(8,128)}) %all-gather.21.cloned.1.call-update) | async-done | bytes 1572880 | tf_op jit(solution)/shard_map/all_gather | solution.py:57
  117.4 50.5 %all-gather.17.cloned.1.call-done = f32[32,4,32,256]{3,2,1,0:T(8,128)} async-done(((f32[4,4,32,256]{3,2,1,0:T(8,128)}), f32[32,4,32,256]{3,2,1,0:T(8,128)}) %all-gather.17.cloned.1.call-update) | async-done | bytes 4194320 | tf_op jit(solution)/shard_map/all_gather | solution.py:57
  167.9 3.5 %fusion.156 = (f32[1,4,32,256]{3,2,1,0:T(8,128)S(1)}, f32[1,4,32,256]{3,2,1,0:T(8,128)S(1)}, f32[1,4,32,256]{3,2,1,0:T(8,128)S(1)}, f32[1,4,32,256]{3,2,1,0:T(8,...) fusion(f32[8,4,4,32,256]{4,3,2,1,0:T(8,128)} %bitcast.750), kind=kLoop, calls=%fused_computation.341 | loop fusion | flops 1409024 | bytes 5898240 | tf_op jit(solution)/shard_map/add | solution.py:176
  175.3 2.4 slice_bitcast_fusion.50
  177.7 3.0 slice_bitcast_fusion.51
  181.0 61.6 %all-gather.11.cloned.1.call-done = f32[8,2,3,4,32,256]{5,4,3,2,1,0:T(8,128)} async-done(((f32[1,2,3,4,32,256]{5,4,3,2,1,0:T(8,128)}), f32[8,2,3,4,32,256]{5,4,3,2,1,0:T(8,128)}) %all-gather.11.cloned.1.call-update) | async-done | bytes 6291472 | tf_op jit(solution)/shard_map/all_gather | solution.py:57
  255.5 3.1 fusion.20
  260.3 8.3 %all-gather.19.cloned.1.call-done = f32[8,4,32,256]{3,2,1,0:T(8,128)} async-done(((f32[4,4,32,256]{3,2,1,0:T(8,128)}), f32[8,4,32,256]{3,2,1,0:T(8,128)}) %all-gather.19.cloned.1.call-update) | async-done | bytes 1048592 | tf_op jit(solution)/shard_map/all_gather | solution.py:57
  268.6 2.3 slice_bitcast_fusion.23
  271.0 5.1 %fusion.10 = f32[2,3,4,32,256]{4,3,2,1,0:T(8,128)S(1)} fusion(f32[1,3,4,32,256]{4,3,2,1,0:T(8,128)} %copy-done.18, f32[1,3,4,32,256]{4,3,2,1,0:T(8,128)} %copy-done.17, f32[8,2,3,4,32,256]{5,4,3,2,1,0:T(8,128)} %all-gather.11.cloned.1.call-done, pred[]{:T(512)S(6)} %gt.45, pred[]{:T(512)S(6)} %gt.44, pred[]{:T(512)S(6)} %gt.43, pred[]{:T(512)S(6)} %gt.42, ...), kind=kLoop, calls=%fused_computation.47 | loop fusion | flops 4718592 | bytes 13369352 | tf_op jit(solution)/shard_map/jit(_where)/select_n | solution.py:62
  276.2 27.3 %all-gather.13.cloned.1.call-done = f32[2,2,3,4,32,256]{5,4,3,2,1,0:T(8,128)} async-done(((f32[1,2,3,4,32,256]{5,4,3,2,1,0:T(8,128)}), f32[2,2,3,4,32,256]{5,4,3,2,1,0:T(8,128)}) %all-gather.13.cloned.1.call-update) | async-done | bytes 1572880 | tf_op jit(solution)/shard_map/all_gather | solution.py:57
  (308 shorter events, 53.7 us)
Async XLA Ops:
  7.2 14.0 %copy-start = (f32[1,3,4,32,256]{4,3,2,1,0:T(8,128)S(1)}, f32[1,3,4,32,256]{4,3,2,1,0:T(8,128)}, u32[]{:S(2)}) copy-start(f32[1,3,4,32,256]{4,3,2,1,0:T(8,128)} %param.18) | copy-start | bytes 1179652
  7.2 84.0 %all-gather.15.cloned.1.call-start = ((), (), s32[]{:S(2)}) async-start(), calls=%async_computation.2 | async-start | bytes 1572864 | tf_op jit(solution)/shard_map/all_gather | solution.py:57
  8.2 16.4 %collective-permute-start.1 = (f32[3,4,1,256]{3,2,1,0:T(1,128)S(1)}, f32[3,4,1,256]{3,2,1,0:T(1,128)S(1)}, u32[]{:S(2)}, u32[]{:S(2)}) collective-permute-start(f32[3,4,1,256]{3,2,1,0:T(1,128)S(1)} %get-tuple-element.230), channel_id=1, source_target_pairs={{0,1},{1,2},{2,3},{3,4},{4,5},{5,6},{6,7},{8,9},{9,10},{10,11},{11... | collective-permute-start | bytes 36872 | tf_op jit(solution)/shard_map/ppermute | solution.py:31
  11.4 15.9 %collective-permute-start = (f32[3,4,1,256]{3,2,1,0:T(1,128)S(1)}, f32[3,4,1,256]{3,2,1,0:T(1,128)S(1)}, u32[]{:S(2)}, u32[]{:S(2)}) collective-permute-start(f32[3,4,1,256]{3,2,1,0:T(1,128)S(1)} %get-tuple-element.229), channel_id=1, source_target_pairs={{1,0},{2,1},{3,2},{4,3},{5,4},{6,5},{7,6},{9,8},{10,9},{11,10},{12... | collective-permute-start | bytes 36872 | tf_op jit(solution)/shard_map/ppermute | solution.py:33
  19.1 8.2 %copy-start.30 = (f32[4,32,256]{2,1,0:T(8,128)S(1)}, f32[4,32,256]{2,1,0:T(8,128)}, u32[]{:S(2)}) copy-start(f32[4,32,256]{2,1,0:T(8,128)} %param.25) | copy-start | bytes 393220
  19.1 8.2 %collective-permute-start.2 = (f32[3,4,1,256]{3,2,1,0:T(1,128)S(1)}, f32[3,4,1,256]{3,2,1,0:T(1,128)S(1)}, u32[]{:S(2)}, u32[]{:S(2)}) collective-permute-start(f32[3,4,1,256]{3,2,1,0:T(1,128)S(1)} %pad_maximum_fusion.18), channel_id=1, source_target_pairs={{0,1},{1,2},{2,3},{3,4},{4,5},{5,6},{6,7},{8,9},{9,10},{10,11},{11... | collective-permute-start | bytes 36872 | tf_op jit(solution)/shard_map/ppermute | solution.py:43
  29.6 9.0 %collective-permute-start.4 = (f32[3,4,1,256]{3,2,1,0:T(1,128)S(1)}, f32[3,4,1,256]{3,2,1,0:T(1,128)S(1)}, u32[]{:S(2)}, u32[]{:S(2)}) collective-permute-start(f32[3,4,1,256]{3,2,1,0:T(1,128)S(1)} %get-tuple-element.224), channel_id=1, source_target_pairs={{0,1},{1,2},{2,3},{3,4},{4,5},{5,6},{6,7},{8,9},{9,10},{10,11},{11... | collective-permute-start | bytes 36872 | tf_op jit(solution)/shard_map/ppermute | solution.py:31
  31.6 7.8 %collective-permute-start.3 = (f32[3,4,1,256]{3,2,1,0:T(1,128)S(1)}, f32[3,4,1,256]{3,2,1,0:T(1,128)S(1)}, u32[]{:S(2)}, u32[]{:S(2)}) collective-permute-start(f32[3,4,1,256]{3,2,1,0:T(1,128)S(1)} %get-tuple-element.223), channel_id=1, source_target_pairs={{1,0},{2,1},{3,2},{4,3},{5,4},{6,5},{7,6},{9,8},{10,9},{11,10},{12... | collective-permute-start | bytes 36872 | tf_op jit(solution)/shard_map/ppermute | solution.py:33
  40.9 9.3 %collective-permute-start.6 = (f32[3,4,1,256]{3,2,1,0:T(1,128)S(1)}, f32[3,4,1,256]{3,2,1,0:T(1,128)S(1)}, u32[]{:S(2)}, u32[]{:S(2)}) collective-permute-start(f32[3,4,1,256]{3,2,1,0:T(1,128)S(1)} %get-tuple-element.218), channel_id=1, source_target_pairs={{0,1},{1,2},{2,3},{3,4},{4,5},{5,6},{6,7},{8,9},{9,10},{10,11},{11... | collective-permute-start | bytes 36872 | tf_op jit(solution)/shard_map/ppermute | solution.py:31
  42.9 8.1 %collective-permute-start.5 = (f32[3,4,1,256]{3,2,1,0:T(1,128)S(1)}, f32[3,4,1,256]{3,2,1,0:T(1,128)S(1)}, u32[]{:S(2)}, u32[]{:S(2)}) collective-permute-start(f32[3,4,1,256]{3,2,1,0:T(1,128)S(1)} %get-tuple-element.217), channel_id=1, source_target_pairs={{1,0},{2,1},{3,2},{4,3},{5,4},{6,5},{7,6},{9,8},{10,9},{11,10},{12... | collective-permute-start | bytes 36872 | tf_op jit(solution)/shard_map/ppermute | solution.py:33
  52.5 9.3 %collective-permute-start.8 = (f32[3,4,1,256]{3,2,1,0:T(1,128)S(1)}, f32[3,4,1,256]{3,2,1,0:T(1,128)S(1)}, u32[]{:S(2)}, u32[]{:S(2)}) collective-permute-start(f32[3,4,1,256]{3,2,1,0:T(1,128)S(1)} %get-tuple-element.212), channel_id=1, source_target_pairs={{0,1},{1,2},{2,3},{3,4},{4,5},{5,6},{6,7},{8,9},{9,10},{10,11},{11... | collective-permute-start | bytes 36872 | tf_op jit(solution)/shard_map/ppermute | solution.py:31
  54.6 8.1 %collective-permute-start.7 = (f32[3,4,1,256]{3,2,1,0:T(1,128)S(1)}, f32[3,4,1,256]{3,2,1,0:T(1,128)S(1)}, u32[]{:S(2)}, u32[]{:S(2)}) collective-permute-start(f32[3,4,1,256]{3,2,1,0:T(1,128)S(1)} %get-tuple-element.211), channel_id=1, source_target_pairs={{1,0},{2,1},{3,2},{4,3},{5,4},{6,5},{7,6},{9,8},{10,9},{11,10},{12... | collective-permute-start | bytes 36872 | tf_op jit(solution)/shard_map/ppermute | solution.py:33
  64.1 22.4 %collective-permute-start.9 = (f32[3,3,4,32,256]{4,3,2,1,0:T(8,128)S(1)}, f32[3,3,4,32,256]{4,3,2,1,0:T(8,128)}, u32[]{:S(2)}, u32[]{:S(2)}) collective-permute-start(f32[3,3,4,32,256]{4,3,2,1,0:T(8,128)S(1)} %pad_maximum_fusion), channel_id=1, source_target_pairs={{0,8},{8,16},{16,24},{24,32},{32,40},{40,48},{48,56},{56,64},{64,7... | collective-permute-start | bytes 3538952 | tf_op jit(solution)/shard_map/ppermute | solution.py:43
  74.4 36.2 %all-gather.21.cloned.1.call-start = ((), (), s32[]{:S(2)}) async-start(), calls=%async_computation.5 | async-start | bytes 2359296 | tf_op jit(solution)/shard_map/all_gather | solution.py:57
  90.1 77.8 %all-gather.17.cloned.1.call-start = ((), (), s32[]{:S(2)}) async-start(), calls=%async_computation.3 | async-start | bytes 4718592 | tf_op jit(solution)/shard_map/all_gather | solution.py:57
  94.6 148.0 %all-gather.11.cloned.1.call-start = ((), (), s32[]{:S(2)}) async-start(), calls=%async_computation | async-start | bytes 7077888 | tf_op jit(solution)/shard_map/all_gather | solution.py:57
  114.9 153.7 %all-gather.19.cloned.1.call-start = ((), (), s32[]{:S(2)}) async-start(), calls=%async_computation.4 | async-start | bytes 1572864 | tf_op jit(solution)/shard_map/all_gather | solution.py:57
  180.7 122.8 %all-gather.13.cloned.1.call-start = ((), (), s32[]{:S(2)}) async-start(), calls=%async_computation.1 | async-start | bytes 2359296 | tf_op jit(solution)/shard_map/all_gather | solution.py:57
  270.9 5.1 %copy-start.75 = (f32[4,32,256]{2,1,0:T(8,128)S(1)}, f32[4,32,256]{2,1,0:T(8,128)}, u32[]{:S(2)}) copy-start(f32[4,32,256]{2,1,0:T(8,128)} %get-tuple-element.192) | copy-start | bytes 393220
  270.9 5.1 %copy-start.76 = (f32[4,32,256]{2,1,0:T(8,128)S(1)}, f32[4,32,256]{2,1,0:T(8,128)}, u32[]{:S(2)}) copy-start(f32[4,32,256]{2,1,0:T(8,128)} %get-tuple-element.193) | copy-start | bytes 393220
  270.9 5.1 %copy-start.77 = (f32[4,32,256]{2,1,0:T(8,128)S(1)}, f32[4,32,256]{2,1,0:T(8,128)}, u32[]{:S(2)}) copy-start(f32[4,32,256]{2,1,0:T(8,128)} %get-tuple-element.194) | copy-start | bytes 393220
  270.9 5.1 %copy-start.78 = (f32[4,32,256]{2,1,0:T(8,128)S(1)}, f32[4,32,256]{2,1,0:T(8,128)}, u32[]{:S(2)}) copy-start(f32[4,32,256]{2,1,0:T(8,128)} %get-tuple-element.195) | copy-start | bytes 393220
  276.0 27.5 %copy-start.50 = (f32[4,32,256]{2,1,0:T(8,128)S(1)}, f32[4,32,256]{2,1,0:T(8,128)}, u32[]{:S(2)}) copy-start(f32[4,32,256]{2,1,0:T(8,128)} %get-tuple-element.144) | copy-start | bytes 393220
  276.0 27.6 %copy-start.49 = (f32[4,32,256]{2,1,0:T(8,128)S(1)}, f32[4,32,256]{2,1,0:T(8,128)}, u32[]{:S(2)}) copy-start(f32[4,32,256]{2,1,0:T(8,128)} %get-tuple-element.142) | copy-start | bytes 393220
  (74 other events, 111.4 us)
Sparse Core Ops, SparseCore 0:
  74.5 16.6 all-gather.14
  93.0 17.6 all-gather.20
  112.4 55.4 all-gather.16
  169.5 73.0 all-gather.10
  244.2 24.3 all-gather.18
  270.2 33.2 all-gather.12
where the time goes:
time: 319 us; the launch traced here: 316 us
  waiting for transfers between devices  180 us (56%)
  other arithmetic  50.5 us (16%)
  starting transfers between devices  47.8 us (15%)
  local copies, waits for them, and re-layouts  22 us (7%)
  between operations  15.7 us (5%)
    all_gather x6, waiting for transfers between devices, entering(): pieces = jax.tree.map(lambda part: lax.all_gather(part, axis), running)  164 us
    ppermute x4, starting transfers between devices, with_halo(): lax.ppermute(head, axis, [((i + 1) % count, i) for i in range(ends)])  27.1 us
    unnamed x164, local copies, waits for them, and re-layouts  14.7 us
    ppermute x2, waiting for transfers between devices, from_behind(): lax.ppermute(value, axis, [(source, source + steps) for source in range(l...  14.5 us
    ppermute x2, starting transfers between devices, from_behind(): lax.ppermute(value, axis, [(source, source + steps) for source in range(l...  11.3 us
    select_n x5, other arithmetic, entering(): jnp.where(passed, new, old)  11 us
    ppermute x4, starting transfers between devices, with_halo(): lax.ppermute(tail, axis, [(i, (i + 1) % count) for i in range(ends)])  8.96 us
    add x12, other arithmetic, combine(): apply_map(latter[0], earlier[1]) + latter[1]  8.77 us
  transfers between devices with their start and end apart: 16, of which 11 were waited for; matrix products, arithmetic and copies ran while one was open for 15% of the time, Pallas kernels for 0%

commit v1 on v0

v1 whole, which is shorter than its diff:
```python
import functools
import math

import jax
import jax.numpy as jnp
from jax import lax
from jax.experimental import pallas as pl
from jax.experimental.pallas import tpu as pltpu
from jax.sharding import PartitionSpec as P

MESH = pl.DeviceIdType.MESH
STEPS = 4
BLK_CIR = 32
AX = 0.22
RA = 0.12
CENTER = 2.0 * (AX + AX + RA)
SHARE = 0.6
F32 = jnp.float32
CHIPS = 16

INNER = (0, 4)
OUTER = (4, 7)


def expand(fam):
    col = lax.broadcasted_iota(jnp.int32, (8, 256), 1) // BLK_CIR
    row = lax.broadcasted_iota(jnp.int32, (8, 256), 0)
    return jnp.dot(
        fam.astype(F32), (col == row).astype(F32), preferred_element_type=F32
    )


def gmatrix(w, im, dp, fs):
    k = im * (CENTER + 2.0 * fs * w)
    hc = 2.0 * dp
    hk = 4.0 * k
    inv = 1.0 / (1.0 + hc + hk)
    return ((1.0 + hc - hk) * inv, 4.0 * inv, -hk * inv, (1.0 - hc - hk) * inv)


def kernel(
    sd, sv, sq, ini, im, dp, vr, fs, fam, prs,
    o_d, o_v, o_q,
    U, V, Q, M, T, SG, WT, FM, IT, Y, Z, S, R, B, NR, E, QE,
    ld, hs, hr, xs, xr, fsd, frc, bs, br, es, er, qs, qr,
):
    t = lax.axis_index("tm")
    sp = lax.axis_index("space")
    me = t // 2
    a = t % 2
    buddy = {"tm": me * 2 + (1 - a)}
    half = pl.ds(pl.multiple_of(a * 128, 128), 128)
    other = pl.ds(pl.multiple_of((1 - a) * 128, 128), 128)

    loads = []

    def load(src, dst):
        c = pltpu.make_async_copy(src, dst, ld.at[len(loads)])
        c.start()
        loads.append(c)

    for slot, src in ((slice(0, 4), slice(0, 4)), (4, 3), (6, 0)):
        load(sd.at[:, :, src], U.at[0, :, pl.ds(1, 4), slot])
        load(sv.at[:, src], V.at[0, :, slot])
        load(sq.at[:, src], Q.at[:, slot])
        for i, m in enumerate((im, dp, vr, fs)):
            load(m.at[:, src], M.at[i, :, slot])
    load(fam, FM.at[0])
    rad_m, g_m = me // 4, me % 4
    load(ini.at[pl.ds(0, 6), rad_m, g_m], IT)

    bar = pltpu.get_barrier_semaphore()

    def greet(k, _):
        d = lax.rem(me + k, CHIPS)
        pl.semaphore_signal(bar, inc=1, device_id={"tm": d * 2 + a}, device_id_type=MESH)
        return 0

    lax.fori_loop(1, CHIPS, greet, 0)
    pl.semaphore_signal(bar, inc=1, device_id=buddy, device_id_type=MESH)
    chain = jnp.logical_or(
        jnp.logical_and(a == 1, t < 31), jnp.logical_and(a == 0, t > 0)
    )
    mate = {"tm": jnp.where(a == 1, t + 1, t - 1)}

    @pl.when(chain)
    def _():
        pl.semaphore_signal(bar, inc=1, device_id=mate, device_id_type=MESH)

    @pl.when(sp > 0)
    def _():
        pl.semaphore_signal(bar, inc=1, device_id={"space": sp - 1}, device_id_type=MESH)

    @pl.when(sp < 7)
    def _():
        pl.semaphore_signal(bar, inc=1, device_id={"space": sp + 1}, device_id_type=MESH)

    zero = jnp.zeros((8, 256), F32)

    def clear(i, _):
        for s in range(STEPS):
            for c in range(3):
                U[s, c, 0, i] = zero
                U[s, c, 5, i] = zero
        return 0

    lax.fori_loop(0, 7, clear, 0)

    for edge, rows in ((7, slice(0, 4)), (0, slice(4, 8))):

        @pl.when(sp == edge)
        def _(rows=rows):
            blank = jnp.zeros((4, 256), F32)
            for c in range(3):
                for r in range(4):
                    U[0, c, r + 1, 5, rows] = blank
                    V[0, c * 4 + r, 5, rows] = blank
                    Q[c * 4 + r, 5, rows] = blank
            for i in range(4):
                for r in range(4):
                    M[i, r, 5, rows] = blank

    greeted = 16 + jnp.where(chain, 1, 0) + jnp.where(sp > 0, 1, 0) + jnp.where(sp < 7, 1, 0)
    pl.semaphore_wait(bar, greeted)

    def halo(side):
        grp, rows, to = ((0, pl.ds(0, 4), sp - 1), (3, pl.ds(4, 4), sp + 1))[side]
        pairs = [
            (sd.at[:, :, grp, rows], U.at[0, :, pl.ds(1, 4), 5, rows]),
            (sv.at[:, grp, rows], V.at[0, :, 5, rows]),
            (sq.at[:, grp, rows], Q.at[:, 5, rows]),
        ]
        for i, m in enumerate((im, dp, vr, fs)):
            pairs.append((m.at[:, grp, rows], M.at[i, :, 5, rows]))
        pairs.append((fam, FM.at[1 + side]))
        return [
            pltpu.make_async_remote_copy(
                src_ref=src, dst_ref=dst, send_sem=hs.at[side, i], recv_sem=hr.at[side, i],
                device_id={"space": to}, device_id_type=MESH,
            )
            for i, (src, dst) in enumerate(pairs)
        ]

    has_from = (sp < 7, sp > 0)
    has_to = (sp > 0, sp < 7)
    for side in (0, 1):

        @pl.when(has_to[side])
        def _(side=side):
            for c in halo(side):
                c.start()

    for c in loads:
        c.wait()

    sub = lax.broadcasted_iota(jnp.int32, (8, 256), 0)

    def following(x, n):
        return jnp.where(sub == 7, pltpu.roll(n, 7, 0), pltpu.roll(x, 7, 0))

    def preceding(x, p):
        return jnp.where(sub == 0, pltpu.roll(p, 1, 0), pltpu.roll(x, 1, 0))

    def after(x):
        return pltpu.roll(x, 255, 1)

    def before(x):
        return pltpu.roll(x, 1, 1)

    def angles(slot, first, second):
        f = jnp.where(
            sub < 4, jnp.broadcast_to(first, (8, 256)), jnp.broadcast_to(second, (8, 256))
        )
        wide = f > 1.5
        co = jnp.where(wide, math.cos(0.9), math.cos(0.5)).astype(F32)
        si = jnp.where(wide, math.sin(0.9), math.sin(0.5)).astype(F32)
        odd = jnp.where(wide, f - 2.0, f) > 0.5
        si = jnp.where(odd, -si, si)
        T[0, slot] = co * co
        T[1, slot] = co * si
        T[2, slot] = si * si

    def prepare(lo, hi):
        for p in range(lo, hi):
            b = hi - 1 if p == lo else p - 1
            T[3, p] = preceding(T[0, p], T[0, b])
            T[4, p] = preceding(T[1, p], T[1, b])
            T[5, p] = before(T[1, p])
            T[6, p] = before(T[2, p])

        def decay(p, _):
            for r in range(4):
                M[2, r, p] = jnp.exp(-M[2, r, p])
            return 0

        lax.fori_loop(lo, hi, decay, 0)

    def steps(lo, hi):
        def strains(s, p):
            n = jnp.where(p == hi - 1, lo, p + 1)
            co2, cs, si2 = T[0, p], T[1, p], T[2, p]
            for r in range(4):
                u1 = U[s, 1, r + 1, p]
                u2 = U[s, 2, r + 1, p]
                d1 = following(u1, U[s, 1, r + 1, n]) - u1
                d2 = following(u2, U[s, 2, r + 1, n]) - u2
                e = co2 * d1 + si2 * (after(u2) - u2) + cs * (d2 + (after(u1) - u1))
                w = jnp.exp(e * e)
                SG[r, p] = M[3, r, p] * w * e

                @pl.when(s == 0)
                def _(r=r, w=w):
                    WT[r, p] = w

        def advance(s, p):
            n = jnp.where(p == hi - 1, lo, p + 1)
            b = jnp.where(p == lo, hi - 1, p - 1)
            co2, cs, si2 = T[0, p], T[1, p], T[2, p]
            co2b, csb, csc, si2c = T[3, p], T[4, p], T[5, p], T[6, p]
            for r in range(4):
                sg = SG[r, p]
                sga = preceding(sg, SG[r, b])
                sgc = before(sg)
                force = (
                    None,
                    (co2 * sg - co2b * sga) + (cs * sg - csc * sgc),
                    (cs * sg - csb * sga) + (si2 * sg - si2c * sgc),
                )
                mass, damp, d = M[0, r, p], M[1, r, p], M[2, r, p]
                gain = SHARE * (1.0 - d)
                for c in range(3):
                    u = U[s, c, r + 1, p]
                    near = (
                        following(u, U[s, c, r + 1, n])
                        + preceding(u, U[s, c, r + 1, b])
                        + after(u)
                        + before(u)
                    )
                    el = (
                        AX * near
                        + RA * (U[s, c, r, p] + U[s, c, r + 2, p])
                        - CENTER * u
                    )
                    i = c * 4 + r
                    q = Q[i, p]
                    total = el + q
                    if c:
                        total = total + force[c]
                    elif r == 0:
                        total = total + prs[0, s]
                    v = V[s, i, p]
                    v = v + mass * total - damp * v
                    V[s + 1, i, p] = v
                    U[s + 1, c, r + 1, p] = u + v
                    Q[i, p] = d * q + gain * el

        def one(s, _):
            lax.fori_loop(lo, hi, lambda p, _: (strains(s, p), 0)[1], 0)
            lax.fori_loop(lo, hi, lambda p, _: (advance(s, p), 0)[1], 0)
            return 0

        lax.fori_loop(0, STEPS, one, 0)

    spread = expand(FM[0])
    for g in range(4):
        angles(g, spread[2 * g : 2 * g + 1], spread[2 * g + 1 : 2 * g + 2])
    prepare(*INNER)
    steps(*INNER)

    def joined(g, get):
        if g == 0:
            return jnp.where(sub < 4, get(6), get(0))
        if g == 3:
            return jnp.where(sub < 4, get(3), get(4))
        return get(g)

    def swap(d):
        return pltpu.make_async_remote_copy(
            src_ref=Z.at[d], dst_ref=Y.at[a, d], send_sem=xs.at[d], recv_sem=xr.at[d],
            device_id=buddy, device_id_type=MESH,
        )

    def swapped(d):
        return pltpu.make_async_remote_copy(
            src_ref=Z.at[d], dst_ref=Y.at[1 - a, d], send_sem=xs.at[d], recv_sem=xr.at[d],
            device_id=buddy, device_id_type=MESH,
        )

    first = a == 0

    def maps(g):
        for r in range(4):
            d = r * 4 + g

            def put(j, x, d=d):
                x0, x1 = x[:, :128], x[:, 128:]
                Y[a, d, j] = jnp.where(first, x0, x1)
                Z[d, j] = jnp.where(first, x1, x0)

            w = joined(g, lambda k, r=r: WT[r, k])
            g00, g01, g10, g11 = gmatrix(w, M[0, r, g], M[1, r, g], M[3, r, g])
            put(6, w)
            for c in range(3):
                i = c * 4 + r
                u0, v0 = U[0, c, r + 1, g], V[0, i, g]
                u4 = joined(g, lambda k, c=c, r=r: U[STEPS, c, r + 1, k])
                v4 = joined(g, lambda k, i=i: V[STEPS, i, k])
                put(c, u4 - (g00 * u0 + g01 * v0))
                put(3 + c, v4 - (g10 * u0 + g11 * v0))
                QE[c, r, g] = joined(g, lambda k, i=i: Q[i, k])
            swap(d).start()

    def onward(d):
        return pltpu.make_async_remote_copy(
            src_ref=S.at[d], dst_ref=R.at[me], send_sem=fsd.at[d], recv_sem=frc.at[me],
            device_id={"tm": d * 2 + a}, device_id_type=MESH,
        )

    def compose(early):
        def tile(k, _):
            d = lax.rem(me + k, CHIPS)

            @pl.when((lax.rem((d + 1) // 2, 2) == 1) == early)
            def _():
                swapped(d).wait_recv()
                r, g = d // 4, d % 4
                w1 = Y[1, d, 6]
                g00, g01, g10, g11 = gmatrix(
                    w1, M[0, r, g, :, half], M[1, r, g, :, half], M[3, r, g, :, half]
                )
                S[d, 6] = Y[0, d, 6]
                S[d, 7] = w1
                for c in range(3):
                    cu, cv = Y[0, d, c], Y[0, d, 3 + c]
                    S[d, c] = g00 * cu + g01 * cv + Y[1, d, c]
                    S[d, 3 + c] = g10 * cu + g11 * cv + Y[1, d, 3 + c]

                @pl.when(d != me)
                def _():
                    onward(d).start()

            return 0

        lax.fori_loop(0, CHIPS, tile, 0)

    maps(1)
    maps(2)

    for side in (0, 1):

        @pl.when(has_from[side])
        def _(side=side):
            for c in halo(side):
                c.wait_recv()

    compose(True)

    after_row = expand(FM[1])[0:1]
    before_row = expand(FM[2])[7:8]
    angles(4, spread[6:7], spread[7:8])
    angles(5, after_row, before_row)
    angles(6, spread[0:1], spread[1:2])
    prepare(*OUTER)
    steps(*OUTER)
    maps(0)
    maps(3)
    compose(False)

    def pass_q(to):
        return pltpu.make_async_remote_copy(
            src_ref=QE, dst_ref=o_q, send_sem=qs, recv_sem=qr,
            device_id={"tm": to}, device_id_type=MESH,
        )

    @pl.when(t < 31)
    def _():
        pass_q(t + 1).start()

    @pl.when(t == 0)
    def _():
        c = pltpu.make_async_copy(ini.at[pl.ds(6, 3)], o_q, ld.at[0])
        c.start()
        c.wait()

    mine = [M[i, rad_m, g_m, :, half] for i in (0, 1, 3)]

    def back(c):
        return pltpu.make_async_remote_copy(
            src_ref=B.at[c], dst_ref=NR.at[me], send_sem=bs.at[c], recv_sem=br.at[me],
            device_id={"tm": c * 2 + a}, device_id_type=MESH,
        )

    def arrived_f(c):
        return pltpu.make_async_remote_copy(
            src_ref=S.at[c], dst_ref=R.at[c], send_sem=fsd.at[c], recv_sem=frc.at[c],
            device_id={"tm": c * 2 + a}, device_id_type=MESH,
        )

    def arrived_b(c):
        return pltpu.make_async_remote_copy(
            src_ref=B.at[c], dst_ref=NR.at[c], send_sem=bs.at[c], recv_sem=br.at[c],
            device_id={"tm": c * 2 + a}, device_id_type=MESH,
        )

    for j in range(8):
        R[me, j] = S[me, j]

    def chip(c, now):
        for j in range(6):
            B[c, j] = now[j]

        @pl.when(c != me)
        def _():
            back(c).start()
            arrived_f(c).wait_recv()

        ga = gmatrix(R[c, 6], *mine)
        gb = gmatrix(R[c, 7], *mine)
        us, vs = [], []
        for j in range(3):
            u, v = now[j], now[3 + j]
            u, v = ga[0] * u + ga[1] * v, ga[2] * u + ga[3] * v
            us.append(gb[0] * u + gb[1] * v + R[c, j])
            vs.append(gb[2] * u + gb[3] * v + R[c, 3 + j])
        return tuple(us + vs)

    lax.fori_loop(0, CHIPS, chip, tuple(IT[j, :, half] for j in range(6)))
    for j in range(6):
        NR[me, j] = B[me, j]

    def deliver(d, field):
        out = (o_d, o_v)[field]
        return pltpu.make_async_remote_copy(
            src_ref=E.at[d, pl.ds(3 * field, 3)], dst_ref=out.at[:, d // 4, d % 4, :, half],
            send_sem=es.at[field, d], recv_sem=er.at[field, d],
            device_id=buddy, device_id_type=MESH,
        )

    def delivered(d, field):
        out = (o_d, o_v)[field]
        return pltpu.make_async_remote_copy(
            src_ref=E.at[d, pl.ds(3 * field, 3)], dst_ref=out.at[:, d // 4, d % 4, :, other],
            send_sem=es.at[field, d], recv_sem=er.at[field, d],
            device_id=buddy, device_id_type=MESH,
        )

    def finish(k, _):
        d = lax.rem(me + k, CHIPS)

        @pl.when(d != me)
        def _():
            arrived_b(d).wait_recv()

        r, g = d // 4, d % 4
        ga = gmatrix(
            Y[0, d, 6], M[0, r, g, :, half], M[1, r, g, :, half], M[3, r, g, :, half]
        )
        for j in range(3):
            u, v = NR[d, j], NR[d, 3 + j]
            u1 = ga[0] * u + ga[1] * v + Y[0, d, j]
            v1 = ga[2] * u + ga[3] * v + Y[0, d, 3 + j]
            E[d, j] = jnp.where(first, u1, u)
            E[d, 3 + j] = jnp.where(first, v1, v)
            o_d[j, r, g, :, half] = jnp.where(first, u, u1)
            o_v[j, r, g, :, half] = jnp.where(first, v, v1)
        deliver(d, 0).start()
        deliver(d, 1).start()
        return 0

    lax.fori_loop(0, CHIPS, finish, 0)

    def settle(d, _):
        for f in (0, 1):
            delivered(d, f).wait_recv()
            deliver(d, f).wait_send()
        swap(d).wait_send()

        @pl.when(d != me)
        def _():
            onward(d).wait_send()
            back(d).wait_send()

        return 0

    lax.fori_loop(0, CHIPS, settle, 0)
    for side in (0, 1):

        @pl.when(has_to[side])
        def _(side=side):
            for c in halo(side):
                c.wait_send()

    @pl.when(t < 31)
    def _():
        pass_q(t + 1).wait_send()

    @pl.when(t > 0)
    def _():
        pass_q(t).wait_recv()


def step(
    start_disp, start_vel, start_visc, init_state, inv_mass, damping_rate, visc_rate,
    fiber_stiff, fiber_family, pressure,
):
    any_ = pl.BlockSpec(memory_space=pl.ANY)
    vmem = pl.BlockSpec(memory_space=pltpu.VMEM)
    out = jax.ShapeDtypeStruct((3, 4, 4, 8, 256), F32)
    dma = pltpu.SemaphoreType.DMA
    outs = pl.pallas_call(
        kernel,
        out_shape=(out, out, out),
        in_specs=[any_] * 9 + [pl.BlockSpec(memory_space=pltpu.SMEM)],
        out_specs=(vmem, vmem, vmem),
        scratch_shapes=[
            pltpu.VMEM((STEPS + 1, 3, 6, 7, 8, 256), F32),
            pltpu.VMEM((STEPS + 1, 12, 7, 8, 256), F32),
            pltpu.VMEM((12, 7, 8, 256), F32),
            pltpu.VMEM((4, 4, 7, 8, 256), F32),
            pltpu.VMEM((7, 7, 8, 256), F32),
            pltpu.VMEM((4, 7, 8, 256), F32),
            pltpu.VMEM((4, 7, 8, 256), F32),
            pltpu.VMEM((3, 8, 8), jnp.int32),
            pltpu.VMEM((6, 8, 256), F32),
            pltpu.VMEM((2, 16, 7, 8, 128), F32),
            pltpu.VMEM((16, 7, 8, 128), F32),
            pltpu.VMEM((16, 8, 8, 128), F32),
            pltpu.VMEM((16, 8, 8, 128), F32),
            pltpu.VMEM((16, 6, 8, 128), F32),
            pltpu.VMEM((16, 6, 8, 128), F32),
            pltpu.VMEM((16, 6, 8, 128), F32),
            pltpu.VMEM((3, 4, 4, 8, 256), F32),
            dma((24,)), dma((2, 8)), dma((2, 8)), dma((16,)), dma((16,)), dma((16,)), dma((16,)),
            dma((16,)), dma((16,)), dma((2, 16)), dma((2, 16)), dma(()), dma(()),
        ],
        compiler_params=pltpu.CompilerParams(
            collective_id=0, has_side_effects=True, vmem_limit_bytes=40 * 1024 * 1024
        ),
    )(
        start_disp.reshape(3, 4, 4, 8, 256),
        start_vel.reshape(12, 4, 8, 256),
        start_visc.reshape(12, 4, 8, 256),
        init_state.reshape(9, 4, 4, 8, 256),
        inv_mass.reshape(4, 4, 8, 256),
        damping_rate.reshape(4, 4, 8, 256),
        visc_rate.reshape(4, 4, 8, 256),
        fiber_stiff.reshape(4, 4, 8, 256),
        fiber_family,
        pressure,
    )
    return tuple(x.reshape(1, 3, 4, 32, 256) for x in outs)


def solution(mesh):
    state = P("tm", None, None, "space", None)
    cell = P(None, "space", None)
    return jax.shard_map(
        step,
        mesh=mesh,
        in_specs=(
            state, state, state, P(None, None, None, "space", None),
            cell, cell, cell, cell, P("space", None), P("tm", None),
        ),
        out_specs=(state, state, state),
        check_vma=False,
    )
```

time: 319 us -> 68.7 us (0.22)
  waiting for transfers between devices: 180 us -> 0 us
  Pallas kernels: 0 us -> 56.3 us
  other arithmetic: 50.5 us -> 0 us
  starting transfers between devices: 47.8 us -> 0 us
  between operations: 15.7 us -> 0.66 us
  local copies, waits for them, and re-layouts: 22 us -> 11.4 us
    all_gather x6 -> x0, waiting for transfers between devices: 164 us -> none  [entering(): pieces = jax.tree.map(lambda part: lax.all_gather(part, axis), running)]
    pallas_call x0 -> x1, Pallas kernels: none -> 56.3 us  [step(): pl.pallas_call(kernel, out_shape=(out, out, out), in_specs=[any_] * 9 + [...]
    ppermute x10 -> x0, starting transfers between devices: 47.4 us -> none  [the longest x4 27.1 us: with_halo(): lax.ppermute(head, axis, [((i + 1) % count, i) for i in range(ends)])]
    add x36 -> x0, other arithmetic: 20.9 us -> none  [the longest x12 8.77 us: combine(): apply_map(latter[0], earlier[1]) + latter[1]]
    ppermute x10 -> x0, waiting for transfers between devices: 16.1 us -> none  [the longest x2 14.5 us: from_behind(): lax.ppermute(value, axis, [(source, source + steps) for source in range(l...]
    select_n x6 -> x0, other arithmetic: 12.5 us -> none  [the longest x5 11 us: entering(): jnp.where(passed, new, old)]
    mul x13 -> x0, other arithmetic: 10.1 us -> none  [the longest x5 7.18 us: apply_map(): gmat[0] * pair[0] + gmat[1] * pair[1]]
    another operation x11 -> x0, other arithmetic: 4.9 us -> none  [the longest x1 1.01 us: apply_map(): jnp.stack([gmat[0] * pair[0] + gmat[1] * pair[1], gmat[2] * pair[0] + gma...]
  transfers between devices with their start and end apart: 16 -> 0, of which waited for: 11 -> 0; matrix products, arithmetic and copies ran while one was open for 15% -> 0% of each run, Pallas kernels for 0% -> 0%
where the time goes in v1:
time: 68.7 us; the launch traced here: 68.4 us
  Pallas kernels  56.3 us (82%)
  local copies, waits for them, and re-layouts  11.4 us (17%)
    pallas_call x1, Pallas kernels, step(): pl.pallas_call(kernel, out_shape=(out, out, out), in_specs=[any_] * 9 + [...  56.3 us
    unnamed x23, local copies, waits for them, and re-layouts  11.4 us

profile of v1, /device:TPU:7, one launch (start us, length us, event | category | flops | bytes accessed | tf_op | source)
XLA Modules:
  0.0 68.4 jit_solution(15245430961621728113)
XLA Ops:
  0.6 0.0 copy-start
  0.6 1.3 %copy-done = f32[3,3,4,32,256]{4,3,2,1,0:T(8,128)S(1)} copy-done((f32[3,3,4,32,256]{4,3,2,1,0:T(8,128)S(1)}, f32[3,3,4,32,256]{4,3,2,1,0:T(8,128)}, u32[]{:S(2)}) %copy-start) | copy-done | bytes 1179672
  1.9 0.0 copy-start.1
  1.9 1.0 %copy-done.1 = f32[1,3,4,32,256]{4,3,2,1,0:T(8,128)S(1)} copy-done((f32[1,3,4,32,256]{4,3,2,1,0:T(8,128)S(1)}, f32[1,3,4,32,256]{4,3,2,1,0:T(8,128)}, u32[]{:S(2)}) %copy-start.1) | copy-done | bytes 393240
  2.9 0.0 copy-start.2
  2.9 1.0 %copy-done.2 = f32[1,3,4,32,256]{4,3,2,1,0:T(8,128)S(1)} copy-done((f32[1,3,4,32,256]{4,3,2,1,0:T(8,128)S(1)}, f32[1,3,4,32,256]{4,3,2,1,0:T(8,128)}, u32[]{:S(2)}) %copy-start.2) | copy-done | bytes 393240
  3.9 0.0 copy-start.3
  3.9 1.0 %copy-done.3 = f32[1,3,4,32,256]{4,3,2,1,0:T(8,128)S(1)} copy-done((f32[1,3,4,32,256]{4,3,2,1,0:T(8,128)S(1)}, f32[1,3,4,32,256]{4,3,2,1,0:T(8,128)}, u32[]{:S(2)}) %copy-start.3) | copy-done | bytes 393240
  4.9 0.0 copy-start.4
  4.9 0.9 %copy-done.4 = f32[4,32,256]{2,1,0:T(8,128)S(1)} copy-done((f32[4,32,256]{2,1,0:T(8,128)S(1)}, f32[4,32,256]{2,1,0:T(8,128)}, u32[]{:S(2)}) %copy-start.4) | copy-done | bytes 131096
  5.8 0.0 copy-start.5
  5.8 0.9 %copy-done.5 = f32[4,32,256]{2,1,0:T(8,128)S(1)} copy-done((f32[4,32,256]{2,1,0:T(8,128)S(1)}, f32[4,32,256]{2,1,0:T(8,128)}, u32[]{:S(2)}) %copy-start.5) | copy-done | bytes 131096
  6.7 0.0 copy-start.6
  6.7 0.9 %copy-done.6 = f32[4,32,256]{2,1,0:T(8,128)S(1)} copy-done((f32[4,32,256]{2,1,0:T(8,128)S(1)}, f32[4,32,256]{2,1,0:T(8,128)}, u32[]{:S(2)}) %copy-start.6) | copy-done | bytes 131096
  7.6 0.0 copy-start.7
  7.6 0.9 %copy-done.7 = f32[4,32,256]{2,1,0:T(8,128)S(1)} copy-done((f32[4,32,256]{2,1,0:T(8,128)S(1)}, f32[4,32,256]{2,1,0:T(8,128)}, u32[]{:S(2)}) %copy-start.7) | copy-done | bytes 131096
  8.5 0.0 copy-start.8
  8.5 0.7 %copy-done.8 = s32[8,8]{1,0:T(8,128)S(1)} copy-done((s32[8,8]{1,0:T(8,128)S(1)}, s32[8,8]{1,0:T(8,128)}, u32[]{:S(2)}) %copy-start.8) | copy-done | bytes 280
  9.2 0.0 copy-start.9
  9.2 0.7 copy-done.9
  9.9 56.3 %shard_map.121 = (f32[3,4,4,8,256]{4,3,2,1,0:T(8,128)S(1)}, f32[3,4,4,8,256]{4,3,2,1,0:T(8,128)S(1)}, f32[3,4,4,8,256]{4,3,2,1,0:T(8,128)S(1)}) custom-call(f32[3,4,4,8,256]{4,3,2,1,0:T(8,128)S(1)} %bitcast.12, f32[12,4,8,256]{3,2,1,0:T(8,128)S(1)} %bitcast.13, f32[12,4,8,256]{3,2,1,0:T(8,128)S(1)} %bitcast.14, f32[9,4,4,8,256]{4,3,2,1,0:T(8,128)S(1)} %bitcast.11, ...), custom_call_target="tpu_custom_call" | custom-call | tf_op jit(solution)/shard_map/pallas_call | solution.py:510
  66.1 0.7 %copy.16 = f32[1,3,4,32,256]{4,3,2,1,0:T(8,128)} copy(f32[1,3,4,32,256]{4,3,2,1,0:T(8,128)S(1)} %bitcast.17) | data formatting | bytes 786432
  66.9 0.7 %copy.17 = f32[1,3,4,32,256]{4,3,2,1,0:T(8,128)} copy(f32[1,3,4,32,256]{4,3,2,1,0:T(8,128)S(1)} %bitcast.16) | data formatting | bytes 786432
  67.6 0.7 %copy.18 = f32[1,3,4,32,256]{4,3,2,1,0:T(8,128)} copy(f32[1,3,4,32,256]{4,3,2,1,0:T(8,128)S(1)} %bitcast.15) | data formatting | bytes 786432
Async XLA Ops:
  0.6 1.3 %copy-start = (f32[3,3,4,32,256]{4,3,2,1,0:T(8,128)S(1)}, f32[3,3,4,32,256]{4,3,2,1,0:T(8,128)}, u32[]{:S(2)}) copy-start(f32[3,3,4,32,256]{4,3,2,1,0:T(8,128)} %param.13) | copy-start | bytes 3538948
  1.9 1.0 %copy-start.1 = (f32[1,3,4,32,256]{4,3,2,1,0:T(8,128)S(1)}, f32[1,3,4,32,256]{4,3,2,1,0:T(8,128)}, u32[]{:S(2)}) copy-start(f32[1,3,4,32,256]{4,3,2,1,0:T(8,128)} %param.10) | copy-start | bytes 1179652
  2.9 1.0 %copy-start.2 = (f32[1,3,4,32,256]{4,3,2,1,0:T(8,128)S(1)}, f32[1,3,4,32,256]{4,3,2,1,0:T(8,128)}, u32[]{:S(2)}) copy-start(f32[1,3,4,32,256]{4,3,2,1,0:T(8,128)} %param.11) | copy-start | bytes 1179652
  3.9 1.0 %copy-start.3 = (f32[1,3,4,32,256]{4,3,2,1,0:T(8,128)S(1)}, f32[1,3,4,32,256]{4,3,2,1,0:T(8,128)}, u32[]{:S(2)}) copy-start(f32[1,3,4,32,256]{4,3,2,1,0:T(8,128)} %param.12) | copy-start | bytes 1179652
  4.9 0.9 %copy-start.4 = (f32[4,32,256]{2,1,0:T(8,128)S(1)}, f32[4,32,256]{2,1,0:T(8,128)}, u32[]{:S(2)}) copy-start(f32[4,32,256]{2,1,0:T(8,128)} %param.14) | copy-start | bytes 393220
  5.8 0.9 %copy-start.5 = (f32[4,32,256]{2,1,0:T(8,128)S(1)}, f32[4,32,256]{2,1,0:T(8,128)}, u32[]{:S(2)}) copy-start(f32[4,32,256]{2,1,0:T(8,128)} %param.15) | copy-start | bytes 393220
  6.7 0.9 %copy-start.6 = (f32[4,32,256]{2,1,0:T(8,128)S(1)}, f32[4,32,256]{2,1,0:T(8,128)}, u32[]{:S(2)}) copy-start(f32[4,32,256]{2,1,0:T(8,128)} %param.16) | copy-start | bytes 393220
  7.6 0.9 %copy-start.7 = (f32[4,32,256]{2,1,0:T(8,128)S(1)}, f32[4,32,256]{2,1,0:T(8,128)}, u32[]{:S(2)}) copy-start(f32[4,32,256]{2,1,0:T(8,128)} %param.17) | copy-start | bytes 393220
  8.5 0.7 %copy-start.8 = (s32[8,8]{1,0:T(8,128)S(1)}, s32[8,8]{1,0:T(8,128)}, u32[]{:S(2)}) copy-start(s32[8,8]{1,0:T(8,128)} %fam.1) | copy-start | bytes 772
  9.2 0.7 copy-start.9

commit v2 on v1

v2 whole, which is shorter than its diff:
```python
import functools
import math

import jax
import jax.numpy as jnp
from jax import lax
from jax.experimental import pallas as pl
from jax.experimental.pallas import tpu as pltpu
from jax.sharding import PartitionSpec as P

MESH = pl.DeviceIdType.MESH
STEPS = 4
BLK_CIR = 32
AX = 0.22
RA = 0.12
CENTER = 2.0 * (AX + AX + RA)
SHARE = 0.6
F32 = jnp.float32
CHIPS = 16

ROWS = 80
INNER = (1, 5)
OUTER = (6, 9)
EARLY = (0, 6)
LATE = (6, 2)


def expand(fam):
    col = lax.broadcasted_iota(jnp.int32, (8, 256), 1) // BLK_CIR
    row = lax.broadcasted_iota(jnp.int32, (8, 256), 0)
    return jnp.dot(
        fam.astype(F32), (col == row).astype(F32), preferred_element_type=F32
    )


def gmatrix(w, im, dp, fs):
    k = im * (CENTER + 2.0 * fs * w)
    hc = 2.0 * dp
    hk = 4.0 * k
    inv = 1.0 / (1.0 + hc + hk)
    return ((1.0 + hc - hk) * inv, 4.0 * inv, -hk * inv, (1.0 - hc - hk) * inv)


def rows(p, shift=0):
    return pl.ds(8 * p + shift, 8)


def kernel(
    sd, sv, sq, ini, im, dp, vr, fs, fam, prs,
    o_d, o_v, o_q,
    U, V, Q, M, T, SG, W, FM, IT, IQ, PR, Y, Z, S, R, GG, B, NR, O, E,
    ld, hs, hr, xs, xr, fsd, frc, bs, br, es, er, qs, qr, os,
):
    t = lax.axis_index("tm")
    sp = lax.axis_index("space")
    me = t // 2
    a = t % 2
    first = a == 0
    buddy = {"tm": me * 2 + (1 - a)}
    lanes = (pl.ds(0, 128), pl.ds(128, 128))

    loads = []

    def load(src, dst):
        c = pltpu.make_async_copy(src, dst, ld.at[len(loads)])
        c.start()
        loads.append(c)

    states = ((sd, lambda *i: U.at[(0,) + i]), (sv, lambda *i: V.at[(0,) + i]), (sq, lambda *i: Q.at[i]))
    mats = tuple((m, lambda *i, k=k: M.at[(k,) + i]) for k, m in enumerate((im, dp, vr, fs)))
    fields = states + mats
    every = slice(None)
    for h in (0, 1):
        for src, dst in fields:
            load(src.at[:, :, lanes[h]], dst(every, h, pl.ds(8, 32)))
            load(src.at[:, pl.ds(24, 8), lanes[h]], dst(every, h, pl.ds(48, 8)))
            load(src.at[:, pl.ds(0, 8), lanes[h]], dst(every, h, pl.ds(64, 8)))
    load(fam, FM.at[0])
    load(prs, PR)
    rad_m, q_m = me // 4, me % 4
    for h in (0, 1):
        load(ini.at[pl.ds(0, 6), rad_m, :, lanes[h]], IT.at[:, h])

    bar = pltpu.get_barrier_semaphore()

    def greet(k, _):
        d = lax.rem(me + k, CHIPS)
        pl.semaphore_signal(bar, inc=1, device_id={"tm": d * 2 + a}, device_id_type=MESH)
        return 0

    @pl.when(sp > 0)
    def _():
        pl.semaphore_signal(bar, inc=1, device_id={"space": sp - 1}, device_id_type=MESH)

    @pl.when(sp < 7)
    def _():
        pl.semaphore_signal(bar, inc=1, device_id={"space": sp + 1}, device_id_type=MESH)

    lax.fori_loop(1, CHIPS, greet, 0)
    pl.semaphore_signal(bar, inc=1, device_id=buddy, device_id_type=MESH)
    chain = jnp.logical_or(
        jnp.logical_and(a == 1, t < 31), jnp.logical_and(a == 0, t > 0)
    )
    mate = {"tm": jnp.where(a == 1, t + 1, t - 1)}

    @pl.when(chain)
    def _():
        pl.semaphore_signal(bar, inc=1, device_id=mate, device_id_type=MESH)

    for edge, at in ((7, pl.ds(56, 4)), (0, pl.ds(60, 4))):

        @pl.when(sp == edge)
        def _(at=at):
            blank = jnp.zeros((4, 128), F32)
            for h in (0, 1):
                for i in range(12):
                    U[0, i, h, at] = blank
                    V[0, i, h, at] = blank
                    Q[i, h, at] = blank
                for k in range(4):
                    for r in range(4):
                        M[k, r, h, at] = blank

    greeted = 16 + jnp.where(chain, 1, 0) + jnp.where(sp > 0, 1, 0) + jnp.where(sp < 7, 1, 0)
    pl.semaphore_wait(bar, greeted)

    def halo(side):
        cut, at, to = ((pl.ds(0, 4), pl.ds(56, 4), sp - 1), (pl.ds(28, 4), pl.ds(60, 4), sp + 1))[side]
        pairs = [(fam, FM.at[1 + side])]
        for src, dst in fields:
            for h in (0, 1):
                pairs.append((src.at[:, cut, lanes[h]], dst(every, h, at)))
        return [
            pltpu.make_async_remote_copy(
                src_ref=src, dst_ref=dst, send_sem=hs.at[side, i], recv_sem=hr.at[side, i],
                device_id={"space": to}, device_id_type=MESH,
            )
            for i, (src, dst) in enumerate(pairs)
        ]

    has_from = (sp < 7, sp > 0)
    has_to = (sp > 0, sp < 7)
    for side in (0, 1):

        @pl.when(has_to[side])
        def _(side=side):
            for c in halo(side):
                c.start()

    for c in loads:
        c.wait()

    lane = lax.broadcasted_iota(jnp.int32, (8, 128), 1)

    def after(x):
        y = [pltpu.roll(k, 127, 1) for k in x]
        return [jnp.where(lane == 127, y[1 - h], y[h]) for h in (0, 1)]

    def before(x):
        y = [pltpu.roll(k, 1, 1) for k in x]
        return [jnp.where(lane == 0, y[1 - h], y[h]) for h in (0, 1)]

    upper = lax.broadcasted_iota(jnp.int32, (8, 256), 0) < 4

    def angles(p, one, two):
        f = jnp.where(
            upper, jnp.broadcast_to(one, (8, 256)), jnp.broadcast_to(two, (8, 256))
        )
        wide = f > 1.5
        co = jnp.where(wide, math.cos(0.9), math.cos(0.5)).astype(F32)
        si = jnp.where(wide, math.sin(0.9), math.sin(0.5)).astype(F32)
        odd = jnp.where(wide, f - 2.0, f) > 0.5
        si = jnp.where(odd, -si, si)
        co2, cs, si2 = [[x[:, :128], x[:, 128:]] for x in (co * co, co * si, si * si)]
        csc, si2c = before(cs), before(si2)
        for h in (0, 1):
            T[0, h, rows(p)] = co2[h]
            T[1, h, rows(p)] = cs[h]
            T[2, h, rows(p)] = si2[h]
            T[3, h, rows(p)] = co2[h] + cs[h]
            T[4, h, rows(p)] = cs[h] + si2[h]
            T[5, h, rows(p)] = csc[h]
            T[6, h, rows(p)] = si2c[h]

    def prepare(lo, hi):
        def rates(p, _):
            for h in (0, 1):
                for r in range(4):
                    d = jnp.exp(-M[2, r, h, rows(p)])
                    M[2, r, h, rows(p)] = d
                    M[4, r, h, rows(p)] = 1.0 - M[1, r, h, rows(p)]
                    M[5, r, h, rows(p)] = SHARE * (1.0 - d)
            return 0

        lax.fori_loop(lo, hi, rates, 0)

    def both(f):
        return [f(0), f(1)]

    def strains(s, p):
        co2, cs, si2 = [both(lambda h, k=k: T[k, h, rows(p)]) for k in range(3)]
        for r in range(4):
            u1 = both(lambda h: U[s, 4 + r, h, rows(p)])
            u2 = both(lambda h: U[s, 8 + r, h, rows(p)])
            c1, c2 = after(u1), after(u2)
            for h in (0, 1):
                d1 = U[s, 4 + r, h, rows(p, 1)] - u1[h]
                d2 = U[s, 8 + r, h, rows(p, 1)] - u2[h]
                e = co2[h] * d1 + si2[h] * (c2[h] - u2[h]) + cs[h] * (d2 + (c1[h] - u1[h]))
                w = jnp.exp(e * e)
                SG[r, h, rows(p)] = M[3, r, h, rows(p)] * w * e

                @pl.when(s == 0)
                def _(w=w, r=r, h=h):
                    W[r, h, rows(p)] = w

    def advance(s, p):
        for r in range(4):
            sg = both(lambda h: SG[r, h, rows(p)])
            sc = before(sg)
            f1, f2 = [], []
            for h in (0, 1):
                sb = SG[r, h, rows(p, -1)]
                f1.append(
                    T[3, h, rows(p)] * sg[h] - T[0, h, rows(p, -1)] * sb - T[5, h, rows(p)] * sc[h]
                )
                f2.append(
                    T[4, h, rows(p)] * sg[h] - T[1, h, rows(p, -1)] * sb - T[6, h, rows(p)] * sc[h]
                )
            force = (None, f1, f2)
            mass, d, keep, gain = [both(lambda h, k=k: M[k, r, h, rows(p)]) for k in (0, 2, 4, 5)]
            for c in range(3):
                i = c * 4 + r
                u = both(lambda h: U[s, i, h, rows(p)])
                ca, cb = after(u), before(u)
                for h in (0, 1):
                    near = (U[s, i, h, rows(p, 1)] + U[s, i, h, rows(p, -1)]) + (ca[h] + cb[h])
                    radial = U[s, i - 1, h, rows(p)] if r > 0 else U[s, i + 1, h, rows(p)]
                    if 0 < r < 3:
                        radial = radial + U[s, i + 1, h, rows(p)]
                    el = AX * near + RA * radial - CENTER * u[h]
                    q = Q[i, h, rows(p)]
                    total = el + q
                    if c:
                        total = total + force[c][h]
                    elif r == 0:
                        total = total + PR[0, s]
                    v = keep[h] * V[s, i, h, rows(p)] + mass[h] * total
                    V[s + 1, i, h, rows(p)] = v
                    U[s + 1, i, h, rows(p)] = u[h] + v
                    Q[i, h, rows(p)] = d[h] * q + gain[h] * el

    def steps(lo, hi):
        def one(s, _):
            lax.fori_loop(lo, hi, lambda p, _: (strains(s, p), 0)[1], 0)
            lax.fori_loop(lo, hi, lambda p, _: (advance(s, p), 0)[1], 0)
            return 0

        lax.fori_loop(0, STEPS, one, 0)

    spread = expand(FM[0])
    for g in range(4):
        angles(1 + g, spread[2 * g : 2 * g + 1], spread[2 * g + 1 : 2 * g + 2])
    prepare(*INNER)
    steps(*INNER)

    def maps(p):
        for r in range(4):

            def put(j, x, r=r):
                Y[a, j, r, rows(p)] = jnp.where(first, x[0], x[1])
                Z[j, r, rows(p)] = jnp.where(first, x[1], x[0])

            w = both(lambda h: W[r, h, rows(p)])
            g = both(
                lambda h: gmatrix(
                    w[h], M[0, r, h, rows(p)], M[1, r, h, rows(p)], M[3, r, h, rows(p)]
                )
            )
            put(6, w)
            for c in range(3):
                i = c * 4 + r
                cu, cv = [], []
                for h in (0, 1):
                    u0, v0 = U[0, i, h, rows(p)], V[0, i, h, rows(p)]
                    cu.append(U[STEPS, i, h, rows(p)] - (g[h][0] * u0 + g[h][1] * v0))
                    cv.append(V[STEPS, i, h, rows(p)] - (g[h][2] * u0 + g[h][3] * v0))
                put(c, cu)
                put(3 + c, cv)

    stretches = (pl.ds(8, 32), pl.ds(48, 8), pl.ds(64, 8))

    def swap(i, slab):
        return pltpu.make_async_remote_copy(
            src_ref=Z.at[:, :, stretches[i]], dst_ref=Y.at[slab, :, :, stretches[i]],
            send_sem=xs.at[i], recv_sem=xr.at[i], device_id=buddy, device_id_type=MESH,
        )

    def place(part, q):
        if part is EARLY:
            return 12 + 6 * q, 4 + 6 * q
        return jnp.where(q < 2, 64 + 2 * q, 48 + 2 * q), jnp.where(q < 2, 2 * q, 24 + 2 * q)

    def mix(part):
        return 0 if part is EARLY else 1

    def onward(part, d, slot):
        at = pl.ds(*part)
        return pltpu.make_async_remote_copy(
            src_ref=S.at[d, :, at], dst_ref=R.at[slot, :, at],
            send_sem=fsd.at[mix(part), d], recv_sem=frc.at[mix(part), slot],
            device_id={"tm": d * 2 + a}, device_id_type=MESH,
        )

    def compose(part):
        lo, n = part

        def tile(k, _):
            d = lax.rem(me + k, CHIPS)
            r, q = d // 4, d % 4
            at = pl.ds(place(part, q)[0], n)
            w1 = Y[1, 6, r, at]
            g = gmatrix(w1, M[0, r, a, at], M[1, r, a, at], M[3, r, a, at])
            S[d, 6, lo : lo + n] = Y[0, 6, r, at]
            S[d, 7, lo : lo + n] = w1
            for c in range(3):
                cu, cv = Y[0, c, r, at], Y[0, 3 + c, r, at]
                S[d, c, lo : lo + n] = g[0] * cu + g[1] * cv + Y[1, c, r, at]
                S[d, 3 + c, lo : lo + n] = g[2] * cu + g[3] * cv + Y[1, 3 + c, r, at]

            @pl.when(d != me)
            def _():
                onward(part, d, me).start()

            return 0

        lax.fori_loop(1, CHIPS + 1, tile, 0)
        R[me, :, lo : lo + n] = S[me, :, lo : lo + n]

    lax.fori_loop(*INNER, lambda p, _: (maps(p), 0)[1], 0)
    swap(0, a).start()
    swap(0, 1 - a).wait_recv()
    compose(EARLY)

    for side in (0, 1):

        @pl.when(has_from[side])
        def _(side=side):
            for c in halo(side):
                c.wait_recv()

    after_row = expand(FM[1])[0:1]
    before_row = expand(FM[2])[7:8]
    angles(6, spread[6:7], spread[7:8])
    angles(7, after_row, before_row)
    angles(8, spread[0:1], spread[1:2])
    prepare(*OUTER)
    steps(*OUTER)
    lax.fori_loop(0, 2, lambda p, _: (maps(6 + 2 * p), 0)[1], 0)
    for i in (1, 2):
        swap(i, a).start()
    for i in (1, 2):
        swap(i, 1 - a).wait_recv()
    compose(LATE)

    def pass_q(to):
        made = []
        for src, dst, n in ((12, 4, 4), (16, 8, 16), (32, 24, 4), (52, 28, 4), (64, 0, 4)):
            for h in (0, 1):
                i = len(made)
                made.append(
                    pltpu.make_async_remote_copy(
                        src_ref=Q.at[:, h, pl.ds(src, n)], dst_ref=o_q.at[:, pl.ds(dst, n), lanes[h]],
                        send_sem=qs.at[i], recv_sem=qr.at[i], device_id={"tm": to}, device_id_type=MESH,
                    )
                )
        return made

    @pl.when(t < 31)
    def _():
        for c in pass_q(t + 1):
            c.start()

    def back(part, c, slot):
        at = pl.ds(*part)
        return pltpu.make_async_remote_copy(
            src_ref=B.at[c, :, at], dst_ref=NR.at[slot, :, at],
            send_sem=bs.at[mix(part), c], recv_sem=br.at[mix(part), slot],
            device_id={"tm": c * 2 + a}, device_id_type=MESH,
        )

    def recur(part):
        lo, n = part
        at = slice(lo, lo + n)
        work, own = place(part, q_m)
        mine = [M[i, rad_m, a, pl.ds(work, n)] for i in (0, 1, 3)]

        def absorb(k, _):
            c = lax.rem(me + k, CHIPS)

            @pl.when(c != me)
            def _():
                onward(part, c, c).wait_recv()

            ga = gmatrix(R[c, 6, at], *mine)
            gb = gmatrix(R[c, 7, at], *mine)
            GG[c, 0, at] = gb[0] * ga[0] + gb[1] * ga[2]
            GG[c, 1, at] = gb[0] * ga[1] + gb[1] * ga[3]
            GG[c, 2, at] = gb[2] * ga[0] + gb[3] * ga[2]
            GG[c, 3, at] = gb[2] * ga[1] + gb[3] * ga[3]
            return 0

        lax.fori_loop(1, CHIPS + 1, absorb, 0)

        def chip(c, now):
            for j in range(6):
                B[c, j, at] = now[j]

            @pl.when(c != me)
            def _():
                back(part, c, me).start()

            g = [GG[c, j, at] for j in range(4)]
            us = [g[0] * now[j] + g[1] * now[3 + j] + R[c, j, at] for j in range(3)]
            vs = [g[2] * now[j] + g[3] * now[3 + j] + R[c, 3 + j, at] for j in range(3)]
            return tuple(us + vs)

        lax.fori_loop(0, CHIPS, chip, tuple(IT[j, a, pl.ds(own, n)] for j in range(6)))
        NR[me, :, at] = B[me, :, at]

    def finish(part):
        lo, n = part
        at = slice(lo, lo + n)

        def tile(k, _):
            d = lax.rem(me + k, CHIPS)

            @pl.when(d != me)
            def _():
                back(part, d, d).wait_recv()

            r, q = d // 4, d % 4
            work, own = place(part, q)
            work, own = pl.ds(work, n), pl.ds(own, n)
            g = gmatrix(Y[0, 6, r, work], M[0, r, a, work], M[1, r, a, work], M[3, r, a, work])
            for j in range(3):
                u, v = NR[d, j, at], NR[d, 3 + j, at]
                u1 = g[0] * u + g[1] * v + Y[0, j, r, work]
                v1 = g[2] * u + g[3] * v + Y[0, 3 + j, r, work]
                E[j, r, own] = jnp.where(first, u1, u)
                E[3 + j, r, own] = jnp.where(first, v1, v)
                O[j, r, a, own] = jnp.where(first, u, u1)
                O[3 + j, r, a, own] = jnp.where(first, v, v1)
            return 0

        lax.fori_loop(1, CHIPS + 1, tile, 0)

    spans = (pl.ds(8, 16), pl.ds(0, 8), pl.ds(24, 8))

    def deliver(i, h):
        return pltpu.make_async_remote_copy(
            src_ref=E.at[:, :, spans[i]], dst_ref=O.at[:, :, h, spans[i]],
            send_sem=es.at[i], recv_sem=er.at[i], device_id=buddy, device_id_type=MESH,
        )

    recur(EARLY)
    recur(LATE)

    @pl.when(t == 0)
    def _():
        c = pltpu.make_async_copy(ini.at[pl.ds(6, 3)], IQ, ld.at[0])
        c.start()
        c.wait()
        c = pltpu.make_async_copy(IQ, o_q.reshape(3, 4, 32, 256), ld.at[0])
        c.start()
        c.wait()

    finish(EARLY)
    deliver(0, a).start()
    finish(LATE)
    for i in (1, 2):
        deliver(i, a).start()

    def write(f, h, at):
        out = (o_d, o_v)[f]
        return pltpu.make_async_copy(
            O.at[pl.ds(3 * f, 3), :, h], out.at[:, :, :, at], os.at[f, h]
        )

    near = pl.ds(pl.multiple_of(a * 128, 128), 128)
    far = pl.ds(pl.multiple_of((1 - a) * 128, 128), 128)
    for f in (0, 1):
        write(f, a, near).start()
    for i in (0, 1, 2):
        deliver(i, 1 - a).wait_recv()
    for f in (0, 1):
        write(f, 1 - a, far).start()

    def settle(d, _):
        @pl.when(d != me)
        def _():
            for part in (EARLY, LATE):
                onward(part, d, me).wait_send()
                back(part, d, me).wait_send()

        return 0

    lax.fori_loop(0, CHIPS, settle, 0)
    for i in (0, 1, 2):
        swap(i, a).wait_send()
        deliver(i, a).wait_send()
    for side in (0, 1):

        @pl.when(has_to[side])
        def _(side=side):
            for c in halo(side):
                c.wait_send()

    @pl.when(t < 31)
    def _():
        for c in pass_q(t + 1):
            c.wait_send()

    @pl.when(t > 0)
    def _():
        for c in pass_q(t):
            c.wait_recv()

    for f in (0, 1):
        write(f, a, near).wait()
        write(f, 1 - a, far).wait()


def step(
    start_disp, start_vel, start_visc, init_state, inv_mass, damping_rate, visc_rate,
    fiber_stiff, fiber_family, pressure,
):
    hbm = pl.BlockSpec(memory_space=pltpu.HBM)
    out = jax.ShapeDtypeStruct((3, 4, 32, 256), F32)
    dma = pltpu.SemaphoreType.DMA
    outs = pl.pallas_call(
        kernel,
        out_shape=(out, out, jax.ShapeDtypeStruct((12, 32, 256), F32)),
        in_specs=[hbm] * 10,
        out_specs=(hbm, hbm, hbm),
        scratch_shapes=[
            pltpu.VMEM((STEPS + 1, 12, 2, ROWS, 128), F32),
            pltpu.VMEM((STEPS + 1, 12, 2, ROWS, 128), F32),
            pltpu.VMEM((12, 2, ROWS, 128), F32),
            pltpu.VMEM((6, 4, 2, ROWS, 128), F32),
            pltpu.VMEM((7, 2, ROWS, 128), F32),
            pltpu.VMEM((4, 2, ROWS, 128), F32),
            pltpu.VMEM((4, 2, ROWS, 128), F32),
            pltpu.VMEM((3, 8, 8), jnp.int32),
            pltpu.VMEM((6, 2, 32, 128), F32),
            pltpu.VMEM((3, 4, 32, 256), F32),
            pltpu.SMEM((1, 4), F32),
            pltpu.VMEM((2, 7, 4, ROWS, 128), F32),
            pltpu.VMEM((7, 4, ROWS, 128), F32),
            pltpu.VMEM((16, 8, 8, 128), F32),
            pltpu.VMEM((16, 8, 8, 128), F32),
            pltpu.VMEM((16, 4, 8, 128), F32),
            pltpu.VMEM((16, 6, 8, 128), F32),
            pltpu.VMEM((16, 6, 8, 128), F32),
            pltpu.VMEM((6, 4, 2, 32, 128), F32),
            pltpu.VMEM((6, 4, 32, 128), F32),
            dma((46,)), dma((2, 15)), dma((2, 15)), dma((3,)), dma((3,)), dma((2, 16)), dma((2, 16)),
            dma((2, 16)), dma((2, 16)), dma((3,)), dma((3,)), dma((10,)), dma((10,)), dma((2, 2)),
        ],
        compiler_params=pltpu.CompilerParams(
            collective_id=0, has_side_effects=True, vmem_limit_bytes=63 * 1024 * 1024
        ),
    )(
        start_disp.reshape(12, 32, 256),
        start_vel.reshape(12, 32, 256),
        start_visc.reshape(12, 32, 256),
        init_state.reshape(9, 4, 32, 256),
        inv_mass,
        damping_rate,
        visc_rate,
        fiber_stiff,
        fiber_family,
        pressure,
    )
    return tuple(x.reshape(1, 3, 4, 32, 256) for x in outs)


def solution(mesh):
    state = P("tm", None, None, "space", None)
    cell = P(None, "space", None)
    return jax.shard_map(
        step,
        mesh=mesh,
        in_specs=(
            state, state, state, P(None, None, None, "space", None),
            cell, cell, cell, cell, P("space", None), P("tm", None),
        ),
        out_specs=(state, state, state),
        check_vma=False,
    )
```

time: 68.7 us -> 57.4 us (0.84)
  local copies, waits for them, and re-layouts: 11.4 us -> 4.33 us
  Pallas kernels: 56.3 us -> 51.9 us
    unnamed x23 -> x5, local copies, waits for them, and re-layouts: 11.4 us -> 4.33 us
    pallas_call x1, Pallas kernels: 56.3 us -> 51.9 us  [step(): pl.pallas_call(kernel, out_shape=(out, out, jax.ShapeDtypeStruct((12, 32,...]
where the time goes in v2:
time: 57.4 us; the launch traced here: 56.8 us
  Pallas kernels  51.9 us (90%)
  local copies, waits for them, and re-layouts  4.33 us (8%)
  between operations  0.65 us (1%)
    pallas_call x1, Pallas kernels, step(): pl.pallas_call(kernel, out_shape=(out, out, jax.ShapeDtypeStruct((12, 32,...  51.9 us
    unnamed x5, local copies, waits for them, and re-layouts  4.33 us

profile of v2, /device:TPU:7, one launch (start us, length us, event | category | flops | bytes accessed | tf_op | source)
XLA Modules:
  0.0 56.8 jit_solution(6469794834730985209)
XLA Ops:
  0.6 51.9 %shard_map.121 = (f32[3,4,32,256]{3,2,1,0:T(8,128)}, f32[3,4,32,256]{3,2,1,0:T(8,128)}, f32[12,32,256]{2,1,0:T(8,128)}) custom-call(f32[12,32,256]{2,1,0:T(8,128)} %bitcast.8, f32[12,32,256]{2,1,0:T(8,128)} %bitcast.9, f32[12,32,256]{2,1,0:T(8,128)} %bitcast.10, f32[9,4,32,256]{3,2,1,0:T(8,128)} %bitcast.7, f32[4,32,256]{2,1,0:T(8,128)} %im.1, ...), custom_call_target="tpu_custom_call" | custom-call | tf_op jit(solution)/shard_map/pallas_call | solution.py:541
  52.5 0.0 copy-start
  52.5 1.8 %copy.16 = f32[1,3,4,32,256]{4,3,2,1,0:T(8,128)} copy(f32[1,3,4,32,256]{4,3,2,1,0:T(8,128)} %bitcast.13) | data formatting | bytes 786432
  54.3 1.8 %copy.17 = f32[1,3,4,32,256]{4,3,2,1,0:T(8,128)} copy(f32[1,3,4,32,256]{4,3,2,1,0:T(8,128)} %bitcast.12) | data formatting | bytes 786432
  56.1 0.0 copy-done
  56.1 0.7 %copy.18 = f32[1,3,4,32,256]{4,3,2,1,0:T(8,128)} copy(f32[1,3,4,32,256]{4,3,2,1,0:T(8,128)S(1)} %bitcast.11) | data formatting | bytes 786432
Async XLA Ops:
  52.5 3.6 %copy-start = (f32[12,32,256]{2,1,0:T(8,128)S(1)}, f32[12,32,256]{2,1,0:T(8,128)}, u32[]{:S(2)}) copy-start(f32[12,32,256]{2,1,0:T(8,128)} %get-tuple-element.8) | copy-start | bytes 1179652

commit v3 on v2

--- a/solution.py
+++ b/solution.py
@@ -17,6 +17,7 @@
 SHARE = 0.6
 F32 = jnp.float32
 CHIPS = 16
+PAUSE = 1
 
 ROWS = 80
 INNER = (1, 5)
@@ -47,9 +48,9 @@
 
 def kernel(
     sd, sv, sq, ini, im, dp, vr, fs, fam, prs,
-    o_d, o_v, o_q,
-    U, V, Q, M, T, SG, W, FM, IT, IQ, PR, Y, Z, S, R, GG, B, NR, O, E,
-    ld, hs, hr, xs, xr, fsd, frc, bs, br, es, er, qs, qr, os,
+    O, OQ,
+    U, V, Q, M, T, SG, W, FM, IT, PR, Y, Z, S, R, GG, B, NR, E,
+    ld, hs, hr, xs, xr, fsd, frc, bs, br, es, er, qs, qr,
 ):
     t = lax.axis_index("tm")
     sp = lax.axis_index("space")
@@ -59,6 +60,15 @@
     buddy = {"tm": me * 2 + (1 - a)}
     lanes = (pl.ds(0, 128), pl.ds(128, 128))
 
+    def peer(k):
+        i = k - 1
+        j = i // 2
+        hop = (j + 1) // 2
+        along = jnp.where(lax.rem(j, 2) == 1, 4 - hop, 4 + hop)
+        row = lax.rem(me // 8 + 1 - lax.rem(i, 2), 2)
+        return row * 8 + lax.rem(lax.rem(me, 8) + along, 8)
+
+
     loads = []
 
     def load(src, dst):
@@ -73,11 +83,15 @@
     for h in (0, 1):
         for src, dst in fields:
             load(src.at[:, :, lanes[h]], dst(every, h, pl.ds(8, 32)))
-            load(src.at[:, pl.ds(24, 8), lanes[h]], dst(every, h, pl.ds(48, 8)))
-            load(src.at[:, pl.ds(0, 8), lanes[h]], dst(every, h, pl.ds(64, 8)))
     load(fam, FM.at[0])
     load(prs, PR)
     rad_m, q_m = me // 4, me % 4
+    initial = pltpu.make_async_copy(ini.at[pl.ds(6, 3)], OQ.reshape(3, 4, 32, 256), qr.at[0])
+
+    @pl.when(t == 0)
+    def _():
+        initial.start()
+
     for h in (0, 1):
         load(ini.at[pl.ds(0, 6), rad_m, :, lanes[h]], IT.at[:, h])
 
@@ -107,49 +121,8 @@
     def _():
         pl.semaphore_signal(bar, inc=1, device_id=mate, device_id_type=MESH)
 
-    for edge, at in ((7, pl.ds(56, 4)), (0, pl.ds(60, 4))):
-
-        @pl.when(sp == edge)
-        def _(at=at):
-            blank = jnp.zeros((4, 128), F32)
-            for h in (0, 1):
-                for i in range(12):
-                    U[0, i, h, at] = blank
-                    V[0, i, h, at] = blank
-                    Q[i, h, at] = blank
-                for k in range(4):
-                    for r in range(4):
-                        M[k, r, h, at] = blank
-
-    greeted = 16 + jnp.where(chain, 1, 0) + jnp.where(sp > 0, 1, 0) + jnp.where(sp < 7, 1, 0)
-    pl.semaphore_wait(bar, greeted)
-
-    def halo(side):
-        cut, at, to = ((pl.ds(0, 4), pl.ds(56, 4), sp - 1), (pl.ds(28, 4), pl.ds(60, 4), sp + 1))[side]
-        pairs = [(fam, FM.at[1 + side])]
-        for src, dst in fields:
-            for h in (0, 1):
-                pairs.append((src.at[:, cut, lanes[h]], dst(every, h, at)))
-        return [
-            pltpu.make_async_remote_copy(
-                src_ref=src, dst_ref=dst, send_sem=hs.at[side, i], recv_sem=hr.at[side, i],
-                device_id={"space": to}, device_id_type=MESH,
-            )
-            for i, (src, dst) in enumerate(pairs)
-        ]
-
-    has_from = (sp < 7, sp > 0)
-    has_to = (sp > 0, sp < 7)
-    for side in (0, 1):
-
-        @pl.when(has_to[side])
-        def _(side=side):
-            for c in halo(side):
-                c.start()
-
     for c in loads:
         c.wait()
-
     lane = lax.broadcasted_iota(jnp.int32, (8, 128), 1)
 
     def after(x):
@@ -250,19 +223,74 @@
                     U[s + 1, i, h, rows(p)] = u[h] + v
                     Q[i, h, rows(p)] = d[h] * q + gain[h] * el
 
-    def steps(lo, hi):
+    def steps(lo, hi, begin, end):
         def one(s, _):
             lax.fori_loop(lo, hi, lambda p, _: (strains(s, p), 0)[1], 0)
             lax.fori_loop(lo, hi, lambda p, _: (advance(s, p), 0)[1], 0)
             return 0
 
-        lax.fori_loop(0, STEPS, one, 0)
+        lax.fori_loop(begin, end, one, 0)
 
     spread = expand(FM[0])
     for g in range(4):
         angles(1 + g, spread[2 * g : 2 * g + 1], spread[2 * g + 1 : 2 * g + 2])
     prepare(*INNER)
-    steps(*INNER)
+    steps(*INNER, 0, PAUSE)
+
+    greeted = 16 + jnp.where(chain, 1, 0) + jnp.where(sp > 0, 1, 0) + jnp.where(sp < 7, 1, 0)
+    pl.semaphore_wait(bar, greeted)
+
+    def halo(side):
+        cut, at, to = ((pl.ds(0, 4), pl.ds(56, 4), sp - 1), (pl.ds(28, 4), pl.ds(60, 4), sp + 1))[side]
+        pairs = [(fam, FM.at[1 + side])]
+        for src, dst in fields:
+            for h in (0, 1):
+                pairs.append((src.at[:, cut, lanes[h]], dst(every, h, at)))
+        return [
+            pltpu.make_async_remote_copy(
+                src_ref=src, dst_ref=dst, send_sem=hs.at[side, i], recv_sem=hr.at[side, i],
+                device_id={"space": to}, device_id_type=MESH,
+            )
+            for i, (src, dst) in enumerate(pairs)
+        ]
+
+    has_from = (sp < 7, sp > 0)
+    has_to = (sp > 0, sp < 7)
+    for side in (0, 1):
+
+        @pl.when(has_to[side])
+        def _(side=side):
+            for c in halo(side):
+                c.start()
+
+    for edge, at in ((7, pl.ds(56, 4)), (0, pl.ds(60, 4))):
+
+        @pl.when(sp == edge)
+        def _(at=at):
+            blank = jnp.zeros((4, 128), F32)
+            for h in (0, 1):
+                for i in range(12):
+                    U[0, i, h, at] = blank
+                    V[0, i, h, at] = blank
+                    Q[i, h, at] = blank
+                for k in range(4):
+                    for r in range(4):
+                        M[k, r, h, at] = blank
+
+    inner_loads = len(loads)
+    for h in (0, 1):
+        for src, dst in fields:
+            load(src.at[:, pl.ds(24, 8), lanes[h]], dst(every, h, pl.ds(48, 8)))
+            load(src.at[:, pl.ds(0, 8), lanes[h]], dst(every, h, pl.ds(64, 8)))
+
+    steps(*INNER, PAUSE, STEPS)
+
+    def swap(p, slab):
+        at = pl.ds(pl.multiple_of(8 * p, 8), 8)
+        return pltpu.make_async_remote_copy(
+            src_ref=Z.at[:, :, at], dst_ref=Y.at[slab, :, :, at],
+            send_sem=xs.at[p], recv_sem=xr.at[p], device_id=buddy, device_id_type=MESH,
+        )
 
     def maps(p):
         for r in range(4):
@@ -287,14 +315,7 @@
                     cv.append(V[STEPS, i, h, rows(p)] - (g[h][2] * u0 + g[h][3] * v0))
                 put(c, cu)
                 put(3 + c, cv)
-
-    stretches = (pl.ds(8, 32), pl.ds(48, 8), pl.ds(64, 8))
-
-    def swap(i, slab):
-        return pltpu.make_async_remote_copy(
-            src_ref=Z.at[:, :, stretches[i]], dst_ref=Y.at[slab, :, :, stretches[i]],
-            send_sem=xs.at[i], recv_sem=xr.at[i], device_id=buddy, device_id_type=MESH,
-        )
+        swap(p, a).start()
 
     def place(part, q):
         if part is EARLY:
@@ -316,7 +337,7 @@
         lo, n = part
 
         def tile(k, _):
-            d = lax.rem(me + k, CHIPS)
+            d = peer(k)
             r, q = d // 4, d % 4
             at = pl.ds(place(part, q)[0], n)
             w1 = Y[1, 6, r, at]
@@ -338,8 +359,8 @@
         R[me, :, lo : lo + n] = S[me, :, lo : lo + n]
 
     lax.fori_loop(*INNER, lambda p, _: (maps(p), 0)[1], 0)
-    swap(0, a).start()
-    swap(0, 1 - a).wait_recv()
+    for p in range(*INNER):
+        swap(p, 1 - a).wait_recv()
     compose(EARLY)
 
     for side in (0, 1):
@@ -349,18 +370,18 @@
             for c in halo(side):
                 c.wait_recv()
 
+    for c in loads[inner_loads:]:
+        c.wait()
     after_row = expand(FM[1])[0:1]
     before_row = expand(FM[2])[7:8]
     angles(6, spread[6:7], spread[7:8])
     angles(7, after_row, before_row)
     angles(8, spread[0:1], spread[1:2])
     prepare(*OUTER)
-    steps(*OUTER)
+    steps(*OUTER, 0, STEPS)
     lax.fori_loop(0, 2, lambda p, _: (maps(6 + 2 * p), 0)[1], 0)
-    for i in (1, 2):
-        swap(i, a).start()
-    for i in (1, 2):
-        swap(i, 1 - a).wait_recv()
+    for p in (6, 8):
+        swap(p, 1 - a).wait_recv()
     compose(LATE)
 
     def pass_q(to):
@@ -370,16 +391,11 @@
                 i = len(made)
                 made.append(
                     pltpu.make_async_remote_copy(
-                        src_ref=Q.at[:, h, pl.ds(src, n)], dst_ref=o_q.at[:, pl.ds(dst, n), lanes[h]],
+                        src_ref=Q.at[:, h, pl.ds(src, n)], dst_ref=OQ.at[:, pl.ds(dst, n), lanes[h]],
                         send_sem=qs.at[i], recv_sem=qr.at[i], device_id={"tm": to}, device_id_type=MESH,
                     )
                 )
         return made
-
-    @pl.when(t < 31)
-    def _():
-        for c in pass_q(t + 1):
-            c.start()
 
     def back(part, c, slot):
         at = pl.ds(*part)
@@ -396,7 +412,7 @@
         mine = [M[i, rad_m, a, pl.ds(work, n)] for i in (0, 1, 3)]
 
         def absorb(k, _):
-            c = lax.rem(me + k, CHIPS)
+            c = peer(k)
 
             @pl.when(c != me)
             def _():
@@ -416,16 +432,18 @@
             for j in range(6):
                 B[c, j, at] = now[j]
 
-            @pl.when(c != me)
-            def _():
-                back(part, c, me).start()
-
             g = [GG[c, j, at] for j in range(4)]
             us = [g[0] * now[j] + g[1] * now[3 + j] + R[c, j, at] for j in range(3)]
             vs = [g[2] * now[j] + g[3] * now[3 + j] + R[c, 3 + j, at] for j in range(3)]
             return tuple(us + vs)
 
         lax.fori_loop(0, CHIPS, chip, tuple(IT[j, a, pl.ds(own, n)] for j in range(6)))
+
+        def reply(k, _):
+            back(part, peer(k), me).start()
+            return 0
+
+        lax.fori_loop(1, CHIPS, reply, 0)
         NR[me, :, at] = B[me, :, at]
 
     def finish(part):
@@ -433,7 +451,7 @@
         at = slice(lo, lo + n)
 
         def tile(k, _):
-            d = lax.rem(me + k, CHIPS)
+            d = peer(k)
 
             @pl.when(d != me)
             def _():
@@ -463,17 +481,39 @@
             send_sem=es.at[i], recv_sem=er.at[i], device_id=buddy, device_id_type=MESH,
         )
 
+    for p in (1, 2, 3, 4, 6, 8):
+        swap(p, a).wait_send()
+    for side in (0, 1):
+
+        @pl.when(has_to[side])
+        def _(side=side):
+            for c in halo(side):
+                c.wait_send()
+
     recur(EARLY)
     recur(LATE)
 
-    @pl.when(t == 0)
-    def _():
-        c = pltpu.make_async_copy(ini.at[pl.ds(6, 3)], IQ, ld.at[0])
-        c.start()
-        c.wait()
-        c = pltpu.make_async_copy(IQ, o_q.reshape(3, 4, 32, 256), ld.at[0])
-        c.start()
-        c.wait()
+    @pl.when(t < 31)
+    def _():
+        for c in pass_q(t + 1):
+            c.start()
+
+
+    @pl.when(t < 31)
+    def _():
+        for c in pass_q(t + 1):
+            c.wait_send()
+
+    def settle(d, _):
+        @pl.when(d != me)
+        def _():
+            for part in (EARLY, LATE):
+                onward(part, d, me).wait_send()
+
+        return 0
+
+    lax.fori_loop(0, CHIPS, settle, 0)
+
 
     finish(EARLY)
     deliver(0, a).start()
@@ -481,54 +521,45 @@
     for i in (1, 2):
         deliver(i, a).start()
 
-    def write(f, h, at):
-        out = (o_d, o_v)[f]
-        return pltpu.make_async_copy(
-            O.at[pl.ds(3 * f, 3), :, h], out.at[:, :, :, at], os.at[f, h]
-        )
-
-    near = pl.ds(pl.multiple_of(a * 128, 128), 128)
-    far = pl.ds(pl.multiple_of((1 - a) * 128, 128), 128)
-    for f in (0, 1):
-        write(f, a, near).start()
-    for i in (0, 1, 2):
-        deliver(i, 1 - a).wait_recv()
-    for f in (0, 1):
-        write(f, 1 - a, far).start()
-
-    def settle(d, _):
+
+    def sent(d, _):
         @pl.when(d != me)
         def _():
             for part in (EARLY, LATE):
-                onward(part, d, me).wait_send()
                 back(part, d, me).wait_send()
 
         return 0
 
-    lax.fori_loop(0, CHIPS, settle, 0)
+    lax.fori_loop(0, CHIPS, sent, 0)
     for i in (0, 1, 2):
-        swap(i, a).wait_send()
+        deliver(i, 1 - a).wait_recv()
         deliver(i, a).wait_send()
-    for side in (0, 1):
-
-        @pl.when(has_to[side])
-        def _(side=side):
-            for c in halo(side):
-                c.wait_send()
-
-    @pl.when(t < 31)
-    def _():
-        for c in pass_q(t + 1):
-            c.wait_send()
+
+    @pl.when(t == 0)
+    def _():
+        initial.wait()
 
     @pl.when(t > 0)
     def _():
         for c in pass_q(t):
             c.wait_recv()
 
-    for f in (0, 1):
-        write(f, a, near).wait()
-        write(f, 1 - a, far).wait()
+
+def write_out(moved, visc, o_d, o_v, o_q, sem):
+    copies = [pltpu.make_async_copy(visc, o_q, sem.at[4])]
+    for f, out in enumerate((o_d, o_v)):
+        for h in (0, 1):
+            copies.append(
+                pltpu.make_async_copy(
+                    moved.at[pl.ds(3 * f, 3), :, h],
+                    out.at[:, :, :, pl.ds(128 * h, 128)],
+                    sem.at[2 * f + h],
+                )
+            )
+    for c in copies:
+        c.start()
+    for c in copies:
+        c.wait()
 
 
 def step(
@@ -536,13 +567,13 @@
     fiber_stiff, fiber_family, pressure,
 ):
     hbm = pl.BlockSpec(memory_space=pltpu.HBM)
-    out = jax.ShapeDtypeStruct((3, 4, 32, 256), F32)
+    vmem = pl.BlockSpec(memory_space=pltpu.VMEM)
     dma = pltpu.SemaphoreType.DMA
-    outs = pl.pallas_call(
+    moved, visc = pl.pallas_call(
         kernel,
-        out_shape=(out, out, jax.ShapeDtypeStruct((12, 32, 256), F32)),
+        out_shape=(pltpu.VMEM((6, 4, 2, 32, 128), F32), pltpu.VMEM((12, 32, 256), F32)),
         in_specs=[hbm] * 10,
-        out_specs=(hbm, hbm, hbm),
+        out_specs=(vmem, vmem),
         scratch_shapes=[
             pltpu.VMEM((STEPS + 1, 12, 2, ROWS, 128), F32),
             pltpu.VMEM((STEPS + 1, 12, 2, ROWS, 128), F32),
@@ -553,7 +584,6 @@
             pltpu.VMEM((4, 2, ROWS, 128), F32),
             pltpu.VMEM((3, 8, 8), jnp.int32),
             pltpu.VMEM((6, 2, 32, 128), F32),
-            pltpu.VMEM((3, 4, 32, 256), F32),
             pltpu.SMEM((1, 4), F32),
             pltpu.VMEM((2, 7, 4, ROWS, 128), F32),
             pltpu.VMEM((7, 4, ROWS, 128), F32),
@@ -562,13 +592,12 @@
             pltpu.VMEM((16, 4, 8, 128), F32),
             pltpu.VMEM((16, 6, 8, 128), F32),
             pltpu.VMEM((16, 6, 8, 128), F32),
-            pltpu.VMEM((6, 4, 2, 32, 128), F32),
             pltpu.VMEM((6, 4, 32, 128), F32),
-            dma((46,)), dma((2, 15)), dma((2, 15)), dma((3,)), dma((3,)), dma((2, 16)), dma((2, 16)),
-            dma((2, 16)), dma((2, 16)), dma((3,)), dma((3,)), dma((10,)), dma((10,)), dma((2, 2)),
+            dma((46,)), dma((2, 15)), dma((2, 15)), dma((9,)), dma((9,)), dma((2, 16)), dma((2, 16)),
+            dma((2, 16)), dma((2, 16)), dma((3,)), dma((3,)), dma((10,)), dma((10,)),
         ],
         compiler_params=pltpu.CompilerParams(
-            collective_id=0, has_side_effects=True, vmem_limit_bytes=63 * 1024 * 1024
+            collective_id=0, has_side_effects=True, vmem_limit_bytes=61000 * 1024
         ),
     )(
         start_disp.reshape(12, 32, 256),
@@ -582,6 +611,15 @@
         fiber_family,
         pressure,
     )
+    out = jax.ShapeDtypeStruct((3, 4, 32, 256), F32)
+    outs = pl.pallas_call(
+        write_out,
+        out_shape=(out, out, jax.ShapeDtypeStruct((12, 32, 256), F32)),
+        in_specs=[vmem, vmem],
+        out_specs=(hbm, hbm, hbm),
+        scratch_shapes=[dma((5,))],
+        compiler_params=pltpu.CompilerParams(vmem_limit_bytes=8 * 1024 * 1024),
+    )(moved, visc)
     return tuple(x.reshape(1, 3, 4, 32, 256) for x in outs)
 
 

time: 57.4 us -> 49.6 us (0.86)
  local copies, waits for them, and re-layouts: 4.33 us -> 0 us
  Pallas kernels: 51.9 us -> 48.2 us
    unnamed x5 -> x0, local copies, waits for them, and re-layouts: 4.33 us -> none
    pallas_call x1 -> x2, Pallas kernels: 51.9 us -> 48.2 us  [the longest x1 47.2 us: step(): pl.pallas_call(kernel, out_shape=(pltpu.VMEM((6, 4, 2, 32, 128), F32), pl...]
where the time goes in v3:
time: 49.6 us; the launch traced here: 48.9 us
  Pallas kernels  48.2 us (97%)
  between operations  0.64 us (1%)
    pallas_call x1, Pallas kernels, step(): pl.pallas_call(kernel, out_shape=(pltpu.VMEM((6, 4, 2, 32, 128), F32), pl...  47.2 us
    pallas_call x1, Pallas kernels, step(): pl.pallas_call(write_out, out_shape=(out, out, jax.ShapeDtypeStruct((12,...  1.04 us

profile of v3, /device:TPU:7, one launch (start us, length us, event | category | flops | bytes accessed | tf_op | source)
XLA Modules:
  0.0 48.9 jit_solution(1698594923781983016)
XLA Ops:
  0.6 47.2 %shard_map.121 = (f32[6,4,2,32,128]{4,3,2,1,0:T(8,128)S(1)}, f32[12,32,256]{2,1,0:T(8,128)S(1)}) custom-call(f32[12,32,256]{2,1,0:T(8,128)} %bitcast.8, f32[12,32,256]{2,1,0:T(8,128)} %bitcast.9, f32[12,32,256]{2,1,0:T(8,128)} %bitcast.10, f32[9,4,32,256]{3,2,1,0:T(8,128)} %bitcast.7, f32[4,32,256]{2,1,0:T(8,128)} %im.1, f32[4,32,256]{2,1,0:T(8,128)} %dp.1, ...), custom_call_target="tpu_custom_call" | custom-call | tf_op jit(solution)/shard_map/pallas_call | solution.py:572
  47.8 1.0 %shard_map.122 = (f32[3,4,32,256]{3,2,1,0:T(8,128)}, f32[3,4,32,256]{3,2,1,0:T(8,128)}, f32[12,32,256]{2,1,0:T(8,128)}) custom-call(f32[6,4,2,32,128]{4,3,2,1,0:T(8,128)S(1)} %get-tuple-element.8.moved, f32[12,32,256]{2,1,0:T(8,128)S(1)} %get-tuple-element.9.visc), custom_call_target="tpu_custom_call" | custom-call | tf_op jit(solution)/shard_map/pallas_call | solution.py:615

commit v4 on v3

--- a/solution.py
+++ b/solution.py
@@ -18,6 +18,7 @@
 F32 = jnp.float32
 CHIPS = 16
 PAUSE = 1
+WIDE = 3
 
 ROWS = 80
 INNER = (1, 5)
@@ -225,8 +226,8 @@
 
     def steps(lo, hi, begin, end):
         def one(s, _):
-            lax.fori_loop(lo, hi, lambda p, _: (strains(s, p), 0)[1], 0)
-            lax.fori_loop(lo, hi, lambda p, _: (advance(s, p), 0)[1], 0)
+            lax.fori_loop(lo, hi, lambda p, _: (strains(s, p), 0)[1], 0, unroll=2)
+            lax.fori_loop(lo, hi, lambda p, _: (advance(s, p), 0)[1], 0, unroll=2)
             return 0
 
         lax.fori_loop(begin, end, one, 0)
@@ -241,11 +242,13 @@
     pl.semaphore_wait(bar, greeted)
 
     def halo(side):
-        cut, at, to = ((pl.ds(0, 4), pl.ds(56, 4), sp - 1), (pl.ds(28, 4), pl.ds(60, 4), sp + 1))[side]
+        to = (sp - 1, sp + 1)[side]
         pairs = [(fam, FM.at[1 + side])]
-        for src, dst in fields:
+        for i, (src, dst) in enumerate(fields):
+            n = 4 if i in (0, 6) else 3
+            cut, at = ((0, 56), (32 - n, 64 - n))[side]
             for h in (0, 1):
-                pairs.append((src.at[:, cut, lanes[h]], dst(every, h, at)))
+                pairs.append((src.at[:, pl.ds(cut, n), lanes[h]], dst(every, h, pl.ds(at, n))))
         return [
             pltpu.make_async_remote_copy(
                 src_ref=src, dst_ref=dst, send_sem=hs.at[side, i], recv_sem=hr.at[side, i],
@@ -262,26 +265,6 @@
         def _(side=side):
             for c in halo(side):
                 c.start()
-
-    for edge, at in ((7, pl.ds(56, 4)), (0, pl.ds(60, 4))):
-
-        @pl.when(sp == edge)
-        def _(at=at):
-            blank = jnp.zeros((4, 128), F32)
-            for h in (0, 1):
-                for i in range(12):
-                    U[0, i, h, at] = blank
-                    V[0, i, h, at] = blank
-                    Q[i, h, at] = blank
-                for k in range(4):
-                    for r in range(4):
-                        M[k, r, h, at] = blank
-
-    inner_loads = len(loads)
-    for h in (0, 1):
-        for src, dst in fields:
-            load(src.at[:, pl.ds(24, 8), lanes[h]], dst(every, h, pl.ds(48, 8)))
-            load(src.at[:, pl.ds(0, 8), lanes[h]], dst(every, h, pl.ds(64, 8)))
 
     steps(*INNER, PAUSE, STEPS)
 
@@ -336,8 +319,7 @@
     def compose(part):
         lo, n = part
 
-        def tile(k, _):
-            d = peer(k)
+        def tile(d):
             r, q = d // 4, d % 4
             at = pl.ds(place(part, q)[0], n)
             w1 = Y[1, 6, r, at]
@@ -349,16 +331,39 @@
                 S[d, c, lo : lo + n] = g[0] * cu + g[1] * cv + Y[1, c, r, at]
                 S[d, 3 + c, lo : lo + n] = g[2] * cu + g[3] * cv + Y[1, 3 + c, r, at]
 
-            @pl.when(d != me)
-            def _():
+        def batch(i, _):
+            peers = [peer(WIDE * i + j + 1) for j in range(WIDE)]
+            for d in peers:
+                tile(d)
+            for d in peers:
                 onward(part, d, me).start()
-
             return 0
 
-        lax.fori_loop(1, CHIPS + 1, tile, 0)
+        lax.fori_loop(0, 15 // WIDE, batch, 0)
+        tile(me)
         R[me, :, lo : lo + n] = S[me, :, lo : lo + n]
 
     lax.fori_loop(*INNER, lambda p, _: (maps(p), 0)[1], 0)
+    inner_loads = len(loads)
+    for h in (0, 1):
+        for src, dst in fields:
+            load(src.at[:, pl.ds(24, 8), lanes[h]], dst(every, h, pl.ds(48, 8)))
+            load(src.at[:, pl.ds(0, 8), lanes[h]], dst(every, h, pl.ds(64, 8)))
+
+    for edge, at in ((7, pl.ds(56, 4)), (0, pl.ds(60, 4))):
+
+        @pl.when(sp == edge)
+        def _(at=at):
+            blank = jnp.zeros((4, 128), F32)
+            for h in (0, 1):
+                for i in range(12):
+                    U[0, i, h, at] = blank
+                    V[0, i, h, at] = blank
+                    Q[i, h, at] = blank
+                for k in range(4):
+                    for r in range(4):
+                        M[k, r, h, at] = blank
+
     for p in range(*INNER):
         swap(p, 1 - a).wait_recv()
     compose(EARLY)
@@ -411,22 +416,24 @@
         work, own = place(part, q_m)
         mine = [M[i, rad_m, a, pl.ds(work, n)] for i in (0, 1, 3)]
 
-        def absorb(k, _):
-            c = peer(k)
-
-            @pl.when(c != me)
-            def _():
-                onward(part, c, c).wait_recv()
-
+        def absorb(c):
             ga = gmatrix(R[c, 6, at], *mine)
             gb = gmatrix(R[c, 7, at], *mine)
             GG[c, 0, at] = gb[0] * ga[0] + gb[1] * ga[2]
             GG[c, 1, at] = gb[0] * ga[1] + gb[1] * ga[3]
             GG[c, 2, at] = gb[2] * ga[0] + gb[3] * ga[2]
             GG[c, 3, at] = gb[2] * ga[1] + gb[3] * ga[3]
+
+        def batch(i, _):
+            peers = [peer(WIDE * i + j + 1) for j in range(WIDE)]
+            for c in peers:
+                onward(part, c, c).wait_recv()
+            for c in peers:
+                absorb(c)
             return 0
 
-        lax.fori_loop(1, CHIPS + 1, absorb, 0)
+        absorb(me)
+        lax.fori_loop(0, 15 // WIDE, batch, 0)
 
         def chip(c, now):
             for j in range(6):
@@ -437,7 +444,9 @@
             vs = [g[2] * now[j] + g[3] * now[3 + j] + R[c, 3 + j, at] for j in range(3)]
             return tuple(us + vs)
 
-        lax.fori_loop(0, CHIPS, chip, tuple(IT[j, a, pl.ds(own, n)] for j in range(6)))
+        lax.fori_loop(
+            0, CHIPS, chip, tuple(IT[j, a, pl.ds(own, n)] for j in range(6)), unroll=4
+        )
 
         def reply(k, _):
             back(part, peer(k), me).start()
@@ -450,13 +459,7 @@
         lo, n = part
         at = slice(lo, lo + n)
 
-        def tile(k, _):
-            d = peer(k)
-
-            @pl.when(d != me)
-            def _():
-                back(part, d, d).wait_recv()
-
+        def tile(d):
             r, q = d // 4, d % 4
             work, own = place(part, q)
             work, own = pl.ds(work, n), pl.ds(own, n)
@@ -469,9 +472,17 @@
                 E[3 + j, r, own] = jnp.where(first, v1, v)
                 O[j, r, a, own] = jnp.where(first, u, u1)
                 O[3 + j, r, a, own] = jnp.where(first, v, v1)
+
+        def batch(i, _):
+            peers = [peer(WIDE * i + j + 1) for j in range(WIDE)]
+            for d in peers:
+                back(part, d, d).wait_recv()
+            for d in peers:
+                tile(d)
             return 0
 
-        lax.fori_loop(1, CHIPS + 1, tile, 0)
+        tile(me)
+        lax.fori_loop(0, 15 // WIDE, batch, 0)
 
     spans = (pl.ds(8, 16), pl.ds(0, 8), pl.ds(24, 8))
 

time: 49.6 us -> 48.6 us (0.980)
  Pallas kernels: 48.2 us -> 47.2 us
    pallas_call x1, Pallas kernels: 47.2 us -> 46.2 us  [step(): pl.pallas_call(kernel, out_shape=(pltpu.VMEM((6, 4, 2, 32, 128), F32), pl...]
where the time goes in v4:
time: 48.6 us; the launch traced here: 47.8 us
  Pallas kernels  47.2 us (97%)
  between operations  0.64 us (1%)
    pallas_call x1, Pallas kernels, step(): pl.pallas_call(kernel, out_shape=(pltpu.VMEM((6, 4, 2, 32, 128), F32), pl...  46.2 us
    pallas_call x1, Pallas kernels, step(): pl.pallas_call(write_out, out_shape=(out, out, jax.ShapeDtypeStruct((12,...  1.04 us

profile of v4, /device:TPU:7, one launch (start us, length us, event | category | flops | bytes accessed | tf_op | source)
XLA Modules:
  0.0 47.8 jit_solution(545696488323103681)
XLA Ops:
  0.6 46.2 %shard_map.121 = (f32[6,4,2,32,128]{4,3,2,1,0:T(8,128)S(1)}, f32[12,32,256]{2,1,0:T(8,128)S(1)}) custom-call(f32[12,32,256]{2,1,0:T(8,128)} %bitcast.8, f32[12,32,256]{2,1,0:T(8,128)} %bitcast.9, f32[12,32,256]{2,1,0:T(8,128)} %bitcast.10, f32[9,4,32,256]{3,2,1,0:T(8,128)} %bitcast.7, f32[4,32,256]{2,1,0:T(8,128)} %im.1, f32[4,32,256]{2,1,0:T(8,128)} %dp.1, ...), custom_call_target="tpu_custom_call" | custom-call | tf_op jit(solution)/shard_map/pallas_call | solution.py:583
  46.8 1.0 %shard_map.122 = (f32[3,4,32,256]{3,2,1,0:T(8,128)}, f32[3,4,32,256]{3,2,1,0:T(8,128)}, f32[12,32,256]{2,1,0:T(8,128)}) custom-call(f32[6,4,2,32,128]{4,3,2,1,0:T(8,128)S(1)} %get-tuple-element.8.moved, f32[12,32,256]{2,1,0:T(8,128)S(1)} %get-tuple-element.9.visc), custom_call_target="tpu_custom_call" | custom-call | tf_op jit(solution)/shard_map/pallas_call | solution.py:626
